TPU v7x, 256 devices: a whole 4x4x8 slice. The times are simulated.
256 devices in a mesh: dp: 4 (over y), pipe: 4 (over z_hi), tensor: 16 (over x, z_lo, core).
Axes of the slice: x: 4, y: 4, z: 8 (z_hi: 4, z_lo: 2; z = z_hi * 2 + z_lo), core: 2. Of those that a mesh axis runs over, the one named last changes fastest.
Arguments:
- hidden: bfloat16 [4, 2048, 14336], P('pipe', 'dp', 'tensor'), parts along dimension 1, may hold values from -6 to 6
- residual: bfloat16 [4, 2048, 4096], P('pipe', ('dp', 'tensor')), parts along dimension 1, may hold values from -6 to 6
- norm_gain: float32 [4, 4096], P('pipe'), may hold values from 0.5 to 1.5
- down_weight: bfloat16 [4, 14336, 4096], P('pipe', 'tensor'), may hold values from -0.046875 to 0.046875
- qkv_weight: bfloat16 [4, 4096, 6144], P('pipe', None, 'tensor'), may hold values from -0.09375 to 0.09375
Outputs:
- section_output: bfloat16 [4, 2048, 4096], P('pipe', ('dp', 'tensor')), parts along dimension 1
- projections: bfloat16 [4, 2048, 6144], P('pipe', 'dp', 'tensor'), parts along dimension 1
There are 4 independent parts, one for each index of `dp`. A program takes and returns all parts, laid end to end along the dimension named above; an argument that names none is the same for every part. Nothing has to cross between parts.
All inputs are finite; a program needn't handle non-finite values.
Results may differ from a plain program's by a relative error of at most 0.022.
Values may be sent and summed in bfloat16 or wider, within the bound.
No kernel may reach another device: no remote copies, remote signals or barrier semaphores. Data moves between devices by JAX's collectives and lax.ppermute only.
A program may use at most 64 MiB of HBM per device.

v0:
```python
import jax
import jax.numpy as jnp
from jax import lax
from jax.sharding import PartitionSpec as P


def passed_along(value, axis, steps):
    count = lax.axis_size(axis)
    pairs = [(source, (source + steps) % count) for source in range(count)]
    return lax.ppermute(value, axis, pairs)


def normalize(values, gain_row):
    wide = values.astype(jnp.float32)
    scaler = lax.rsqrt(jnp.mean(wide * wide, axis=-1, keepdims=True) + 1e-05)
    return (wide * scaler * gain_row).astype(jnp.bfloat16)


def shards(hidden, residual, norm_gain, down_weight, qkv_weight):
    hidden_rows = hidden[0]
    resid_rows = residual[0]
    gain_row = norm_gain[0]
    down_local = down_weight[0]
    qkv_local = qkv_weight[0]
    tok_rows = resid_rows.shape[0]
    resid_full = lax.all_gather(resid_rows, "tensor", axis=0, tiled=True)
    summed = lax.psum(
        jnp.dot(hidden_rows, down_local, preferred_element_type=jnp.float32).astype(jnp.bfloat16),
        "tensor",
    ).astype(jnp.float32)
    full_rows = (resid_full.astype(jnp.float32) + summed).astype(jnp.bfloat16)
    offset = lax.axis_index("tensor") * tok_rows
    section_output = lax.dynamic_slice_in_dim(full_rows, offset, tok_rows, 0)
    arrived = passed_along(full_rows, "pipe", 1)
    normed = normalize(arrived, gain_row)
    projections = jnp.dot(normed, qkv_local, preferred_element_type=jnp.float32).astype(
        jnp.bfloat16
    )
    return (section_output[None], projections[None])


def solution(mesh):
    return jax.shard_map(
        shards,
        mesh=mesh,
        in_specs=(
            P("pipe", "dp", "tensor"),
            P("pipe", ("dp", "tensor"), None),
            P("pipe", None),
            P("pipe", "tensor", None),
            P("pipe", None, "tensor"),
        ),
        out_specs=(P("pipe", ("dp", "tensor"), None), P("pipe", "dp", "tensor")),
        check_vma=False,
    )
```

profile of v0, /device:TPU:41, one launch (start us, length us, event | category | flops | bytes accessed | tf_op | source)
XLA Modules:
  0.0 408.5 jit_solution(18110407928350033155)
XLA Ops:
  7.2 0.0 copy-start
  7.2 0.0 all-reduce.2.cloned.1.call-start
  7.2 10.0 %fusion.6 = bf16[512,4096]{1,0:T(8,128)(2,1)} fusion(bf16[1,896,4096]{2,1,0:T(8,128)(2,1)} %param.8, bf16[1,512,896]{2,1,0:T(8,128)(2,1)} %param.5), kind=kOutput, calls=%fused_computation.9 | convolution fusion | flops 3760193536 | bytes 12451840 | tf_op jit(solution)/shard_map/dot_general | solution.py:28
  17.2 0.0 all-reduce.2.cloned.1.call-update
  17.2 0.0 all-gather.3.cloned.1.call-start
  17.3 0.7 all-gather.3.cloned.1.call-update
  18.0 136.9 %all-reduce.2.cloned.1.call-done = bf16[512,4096]{1,0:T(8,128)(2,1)} async-done(((bf16[512,4096]{1,0:T(8,128)(2,1)}), bf16[512,4096]{1,0:T(8,128)(2,1)}) %all-reduce.2.cloned.1.call-update) | async-done | bytes 4194320 | tf_op jit(solution)/shard_map/psum | solution.py:27
  154.9 46.5 %all-gather.3.cloned.1.call-done = bf16[1,512,4096]{2,1,0:T(8,128)(2,1)} async-done(((bf16[1,32,4096]{2,1,0:T(8,128)(2,1)}), bf16[1,512,4096]{2,1,0:T(8,128)(2,1)}) %all-gather.3.cloned.1.call-update) | async-done | bytes 4194320 | tf_op jit(solution)/shard_map/all_gather | solution.py:26
  201.4 7.2 %fusion.3 = bf16[512,4096]{1,0:T(8,128)(2,1)} fusion(bf16[512,4096]{1,0:T(8,128)(2,1)} %all-reduce.2.cloned.1.call-done, bf16[1,512,4096]{2,1,0:T(8,128)(2,1)} %all-gather.3.cloned.1.call-done), kind=kLoop, calls=%fused_computation.6 | loop fusion | flops 8388608 | bytes 12582912 | tf_op jit(solution)/shard_map/convert_element_type | solution.py:31
  208.5 0.0 copy-start.1
  208.5 2.3 collective-permute-start
  210.8 1.7 dynamic-slice_bitcast_fusion
  212.5 180.8 %collective-permute-done = bf16[512,4096]{1,0:T(8,128)(2,1)} collective-permute-done((bf16[512,4096]{1,0:T(8,128)(2,1)}, bf16[512,4096]{1,0:T(8,128)(2,1)}, u32[]{:S(2)}, u32[]{:S(2)}) %collective-permute-start) | collective-permute-done | bytes 4194336 | tf_op jit(solution)/shard_map/ppermute | solution.py:10
  393.3 3.1 fusion
  396.4 0.0 copy-done
  396.4 0.0 copy-done.1
  396.4 5.3 %fusion.19 = bf16[1,512,384]{2,1,0:T(8,128)(2,1)} fusion(bf16[1,4096,384]{2,1,0:T(8,128)(2,1)S(1)} %copy-done, bf16[512,4096]{1,0:T(8,128)(2,1)} %collective-permute-done, f32[4096]{0:T(1024)S(1)} %bitcast.23, f32[512]{0:T(512)S(1)} %add_rsqrt_fusion), kind=kOutput, calls=%fused_computation.15 | convolution fusion | flops 1619197952 | bytes 7751680 | tf_op jit(solution)/shard_map/dot_general | solution.py:36
  (1 shorter events, 0.0 us)
Async XLA Ops:
  7.2 389.2 %copy-start = (bf16[1,4096,384]{2,1,0:T(8,128)(2,1)S(1)}, bf16[1,4096,384]{2,1,0:T(8,128)(2,1)}, u32[]{:S(2)}) copy-start(bf16[1,4096,384]{2,1,0:T(8,128)(2,1)} %param.9) | copy-start | bytes 9437188
  7.2 147.7 %all-reduce.2.cloned.1.call-start = ((), (), s32[]{:S(2)}) async-start(), calls=%async_computation | async-start | bytes 8388608 | tf_op jit(solution)/shard_map/psum | solution.py:27
  17.2 184.1 %all-gather.3.cloned.1.call-start = ((), (), s32[]{:S(2)}) async-start(), calls=%async_computation.1 | async-start | bytes 4456448 | tf_op jit(solution)/shard_map/all_gather | solution.py:26
  208.5 187.8 %copy-start.1 = (f32[1,4096]{1,0:T(1,128)S(1)}, f32[1,4096]{1,0:T(1,128)}, u32[]{:S(2)}) copy-start(f32[1,4096]{1,0:T(1,128)} %param.7) | copy-start | bytes 49156
  208.5 184.7 %collective-permute-start = (bf16[512,4096]{1,0:T(8,128)(2,1)}, bf16[512,4096]{1,0:T(8,128)(2,1)}, u32[]{:S(2)}, u32[]{:S(2)}) collective-permute-start(bf16[512,4096]{1,0:T(8,128)(2,1)} %fusion.3), channel_id=1, source_target_pairs={{0,16},{16,32},{32,48},{48,0},{1,17},{17,33},{33,49},{49,1},{2,18}... | collective-permute-start | bytes 12582920 | tf_op jit(solution)/shard_map/ppermute | solution.py:10
Sparse Core Ops, SparseCore 0:
  17.3 137.5 all-reduce.1
  156.7 44.5 all-gather.2
where the time goes:
time: 410 us; the launch traced here: 409 us
  waiting for transfers between devices  365 us (89%)
  matrix products  15.3 us (4%)
  between operations  14.1 us (3%)
  other arithmetic  10.3 us (3%)
    ppermute x1, waiting for transfers between devices, passed_along(): return lax.ppermute(value, axis, pairs)  181 us
    psum x1, waiting for transfers between devices, shards(): lax.psum(jnp.dot(hidden_rows, down_local, preferred_element_type=jnp.floa...  137 us
    all_gather x1, waiting for transfers between devices, shards(): resid_full = lax.all_gather(resid_rows, 'tensor', axis=0, tiled=True)  46.5 us
    dot_general x1, matrix products, shards(): jnp.dot(hidden_rows, down_local, preferred_element_type=jnp.float32)  9.96 us
  transfers between devices with their start and end apart: 3, of which 3 were waited for; matrix products, arithmetic and copies ran while one was open for 0% of the time, Pallas kernels for 0%

commit v1 on v0

v1 whole, which is shorter than its diff:
```python
import functools
import itertools

import jax
import jax.numpy as jnp
from jax import lax
from jax.experimental import pallas as pl
from jax.experimental.pallas import tpu as pltpu
from jax.sharding import Mesh, PartitionSpec as P

CHUNKS = 2
AXES = ("x", "zl", "core")
SIZES = (4, 2, 2)


def move(value, x_mask=(0, 0), z_mask=0, core_mask=0):
    pairs = []
    for x, z, c in itertools.product(*map(range, SIZES)):
        to = ((x ^ x_mask[c]) * 2 + (z ^ z_mask)) * 2 + (c ^ core_mask)
        pairs.append(((x * 2 + z) * 2 + c, to))
    return lax.ppermute(value, AXES, pairs)


first_x = functools.partial(move, x_mask=(1, 3))
second_x = functools.partial(move, x_mask=(3, 1))
swap_z = functools.partial(move, z_mask=1)
swap_core = functools.partial(move, core_mask=1)


TRADES = {"x1": first_x, "x2": second_x, "z": swap_z}


def next_section(value):
    count = lax.axis_size("pipe")
    return lax.ppermute(value, "pipe", [(s, (s + 1) % count) for s in range(count)])


def normalize(values, gain_row):
    wide = values.astype(jnp.float32)
    scaler = lax.rsqrt(jnp.mean(wide * wide, axis=-1, keepdims=True) + 1e-05)
    return (wide * scaler * gain_row).astype(jnp.bfloat16)


def block_ids(orders):
    x, z, core = (lax.axis_index(a) for a in AXES)
    here = (x * 2 + z) * 2 + core
    near, far = 1 + 2 * core, 3 - 2 * core
    masks = ({"x1": near * 4, "x2": far * 4, "z": 2}, {"x1": far * 4, "x2": near * 4, "z": 2})
    ids = []
    for order in orders:
        for other in (0, 1):
            for p in range(8):
                t = here ^ other
                for bit, name in enumerate(reversed(order)):
                    if p >> bit & 1:
                        t = t ^ masks[other][name]
                ids.append(t)
    return jnp.stack(ids).astype(jnp.int32)


def order_kernel(ids, hid_ref, w_ref, theirs_ref, mine_ref, w_out, hid_sem, w_sem):
    rows = hid_ref.shape[0] // (16 * CHUNKS)
    parts = w_sem.shape[0]
    deep = w_ref.shape[0] // parts
    copies = []
    for i in range(parts):
        at = pl.ds(i * deep, deep)
        copies.append(pltpu.make_async_copy(w_ref.at[at, :], w_out.at[at, :], w_sem.at[i]))
    for i in range(16 * CHUNKS):
        k, other, p = i // 16, i // 8 % 2, i % 8
        start = pl.multiple_of((ids[i] * CHUNKS + k) * rows, rows)
        out = theirs_ref if other else mine_ref
        copies.append(
            pltpu.make_async_copy(
                hid_ref.at[pl.ds(start, rows), :],
                out.at[pl.ds((k * 8 + p) * rows, rows), :],
                hid_sem.at[i],
            )
        )
    for c in copies:
        c.start()
    for c in copies:
        c.wait()


def in_exchange_order(ids, hid, w, parts=8):
    rows, depth = hid.shape
    return pl.pallas_call(
        order_kernel,
        out_shape=[jax.ShapeDtypeStruct((rows // 2, depth), jnp.bfloat16)] * 2
        + [jax.ShapeDtypeStruct(w.shape, w.dtype)],
        grid_spec=pltpu.PrefetchScalarGridSpec(
            num_scalar_prefetch=1,
            grid=(1,),
            in_specs=[pl.BlockSpec(memory_space=pltpu.HBM)] * 2,
            out_specs=[pl.BlockSpec(memory_space=pltpu.VMEM)] * 3,
            scratch_shapes=[
                pltpu.SemaphoreType.DMA((16 * CHUNKS,)),
                pltpu.SemaphoreType.DMA((parts,)),
            ],
        ),
        compiler_params=pltpu.CompilerParams(vmem_limit_bytes=12 << 20),
        cost_estimate=pl.CostEstimate(
            flops=0, bytes_accessed=4 * (rows * depth + w.size), transcendentals=0
        ),
    )(ids, hid, w)


def qkv_kernel(slots, ids, *refs):
    n = len(slots)
    parts, w_ref, (out_ref, acc) = refs[:n], refs[n], refs[-2:]
    step = pl.program_id(0)

    @pl.when(step == 0)
    def _():
        acc[...] = jnp.zeros_like(acc)

    lhs = jnp.concatenate([p[...] for p in parts], axis=0)
    acc[...] += jnp.dot(lhs, w_ref[...], preferred_element_type=jnp.float32)

    @pl.when(step == pl.num_programs(0) - 1)
    def _():
        rows = acc.shape[0] // (4 * n)
        if len(refs) > n + 3:
            out_ref[...] = refs[n + 1][...]
        for i, (k, slot) in enumerate(slots):
            for j in range(4):
                start = pl.multiple_of((ids[16 * k + slot + j] * CHUNKS + k) * rows, rows)
                out_ref[pl.ds(start, rows), :] = acc[pl.ds((i * 4 + j) * rows, rows), :].astype(jnp.bfloat16)


def qkv_rows(slots, ids, pieces, w, before=None, tile=1024):
    part, depth = pieces[0].shape
    width = w.shape[1]
    n = len(slots)
    total = CHUNKS * 4 * part
    whole = pl.BlockSpec((total, width), lambda i, ids: (0, 0))
    return pl.pallas_call(
        functools.partial(qkv_kernel, slots),
        out_shape=jax.ShapeDtypeStruct((total, width), jnp.bfloat16),
        grid_spec=pltpu.PrefetchScalarGridSpec(
            num_scalar_prefetch=1,
            grid=(depth // tile,),
            in_specs=[pl.BlockSpec((part, tile), lambda i, ids: (0, i))] * n
            + [pl.BlockSpec((tile, width), lambda i, ids: (i, 0))]
            + [whole] * (before is not None),
            out_specs=whole,
            scratch_shapes=[pltpu.VMEM((n * part, width), jnp.float32)],
        ),
        compiler_params=pltpu.CompilerParams(vmem_limit_bytes=16 << 20),
        cost_estimate=pl.CostEstimate(
            flops=2 * n * part * depth * width,
            bytes_accessed=2 * (n * part * depth + depth * width + total * width),
            transcendentals=0,
        ),
    )(ids, *pieces, w, *([] if before is None else [before]))


def dot_bf16(a, b):
    return jnp.dot(a, b, preferred_element_type=jnp.float32).astype(jnp.bfloat16)


def add(a, b):
    return (a.astype(jnp.float32) + b.astype(jnp.float32)).astype(jnp.bfloat16)


def shards(hidden, residual, norm_gain, down_weight, qkv_weight):
    resid = residual[0]
    gain = norm_gain[0]
    qkv = qkv_weight[0]
    rows = resid.shape[0] // CHUNKS
    halving = (("x1", "x2", "z"), ("z", "x1", "x2"))
    doubling = (("z", "x2", "x1"), ("z", "x2", "x1"))
    theirs, mine, down = in_exchange_order(block_ids(halving), hidden[0], down_weight[0])
    ids = block_ids([order[::-1] for order in doubling])
    rows8 = 8 * rows
    sent = lax.optimization_barrier(dot_bf16(theirs, down))
    pieces = [lax.optimization_barrier(sent[k * rows8 : (k + 1) * rows8]) for k in range(CHUNKS)]
    kept = lax.optimization_barrier(dot_bf16(mine, down))
    cur = [(kept[k * rows8 : (k + 1) * rows8], swap_core(pieces[k])) for k in range(CHUNKS)]
    for i in range(3):
        after = []
        for k, (own, got) in enumerate(cur):
            half = own.shape[0] // 2
            send = add(own[half:], got[half:])
            keep = add(own[:half], got[:half])
            after.append((keep, TRADES[halving[k][i]](send)))
        cur = after
    outs = []
    for k, (own, got) in enumerate(cur):
        base = resid[k * rows : (k + 1) * rows].astype(jnp.float32)
        if k > 0:
            own, got, _ = lax.optimization_barrier((own, got, outs[-1]))
        out = (base + (own.astype(jnp.float32) + got.astype(jnp.float32))).astype(jnp.bfloat16)
        outs.append(lax.optimization_barrier(out))
    gathered = []
    for k, o in enumerate(outs):
        came = next_section(o)
        if k > 0:
            came, _ = lax.optimization_barrier((came, gathered[-1]))
        gathered.append(normalize(came, gain))
    for i in range(2):
        gathered = [
            jnp.concatenate([g, TRADES[doubling[k][i]](g)], axis=0) for k, g in enumerate(gathered)
        ]
    a, b = gathered
    a_far, b_far = (TRADES[doubling[k][2]](g) for k, g in enumerate(gathered))
    proj = qkv_rows(
        ((0, 0), (0, 4), (0, 8), (0, 12)), ids, (a, a_far, swap_core(a), swap_core(a_far)), qkv
    )
    proj = qkv_rows(((1, 0), (1, 8)), ids, (b, swap_core(b)), qkv, proj)
    b_far, proj = lax.optimization_barrier((b_far, proj))
    proj = qkv_rows(((1, 4), (1, 12)), ids, (b_far, swap_core(b_far)), qkv, proj)
    return (jnp.concatenate(outs, axis=0)[None], proj[None])


def solution(mesh):
    fine = Mesh(mesh.devices.reshape((4, 4) + SIZES), ("dp", "pipe") + AXES)
    return jax.shard_map(
        shards,
        mesh=fine,
        in_specs=(
            P("pipe", "dp", AXES),
            P("pipe", ("dp",) + AXES, None),
            P("pipe", None),
            P("pipe", AXES, None),
            P("pipe", None, AXES),
        ),
        out_specs=(P("pipe", ("dp",) + AXES, None), P("pipe", "dp", AXES)),
        check_vma=False,
    )
```

time: 410 us -> 98.3 us (0.24)
  waiting for transfers between devices: 365 us -> 46.8 us
  starting transfers between devices: 2.34 us -> 19.4 us
  Pallas kernels: 0 us -> 15.9 us
  between operations: 14.1 us -> 0.93 us
  matrix products: 15.3 us -> 4.67 us
  other arithmetic: 10.3 us -> 4.2 us
    psum x1 -> x0, waiting for transfers between devices: 137 us -> none  [shards(): lax.psum(jnp.dot(hidden_rows, down_local, preferred_element_type=jnp.floa...]
    ppermute x1 -> x20, waiting for transfers between devices: 181 us -> 46.8 us  [the longest x18 37.3 us: move(): return lax.ppermute(value, AXES, pairs)]
    all_gather x1 -> x0, waiting for transfers between devices: 46.5 us -> none  [shards(): resid_full = lax.all_gather(resid_rows, 'tensor', axis=0, tiled=True)]
    ppermute x1 -> x20, starting transfers between devices: 2.27 us -> 19.4 us  [the longest x18 13.2 us: move(): return lax.ppermute(value, AXES, pairs)]
    pallas_call x0 -> x4, Pallas kernels: none -> 15.9 us  [the longest x3 11.8 us: qkv_rows(): pl.pallas_call(functools.partial(qkv_kernel, slots), out_shape=jax.ShapeD...]
    dot_general x2, matrix products: 15.3 us -> 4.67 us  [dot_bf16(): jnp.dot(a, b, preferred_element_type=jnp.float32).astype(jnp.bfloat16)]
    convert_element_type x1 -> x9, other arithmetic: 7.18 us -> 1.46 us  [the longest x5 1.14 us: add(): return (a.astype(jnp.float32) + b.astype(jnp.float32)).astype(jnp.bfloat16)]
    unnamed x4 -> x10, local copies, waits for them, and re-layouts: 0.01 us -> 4.28 us
  transfers between devices with their start and end apart: 3 -> 20, of which waited for: 3 -> 13; matrix products, arithmetic and copies ran while one was open for 0% -> 6% of each run, Pallas kernels for 0% -> 8%
where the time goes in v1:
time: 98.3 us; the launch traced here: 96.6 us
  waiting for transfers between devices  46.8 us (48%)
  starting transfers between devices  19.4 us (20%)
  Pallas kernels  15.9 us (16%)
  local copies, waits for them, and re-layouts  4.71 us (5%)
  matrix products  4.67 us (5%)
  other arithmetic  4.2 us (4%)
    ppermute x18, waiting for transfers between devices, move(): return lax.ppermute(value, AXES, pairs)  37.3 us
    ppermute x18, starting transfers between devices, move(): return lax.ppermute(value, AXES, pairs)  13.2 us
    pallas_call x3, Pallas kernels, qkv_rows(): pl.pallas_call(functools.partial(qkv_kernel, slots), out_shape=jax.ShapeD...  11.8 us
    ppermute x2, waiting for transfers between devices, next_section(): lax.ppermute(value, 'pipe', [(s, (s + 1) % count) for s in range(count)])  9.48 us
    ppermute x2, starting transfers between devices, next_section(): lax.ppermute(value, 'pipe', [(s, (s + 1) % count) for s in range(count)])  6.13 us
    dot_general x2, matrix products, dot_bf16(): jnp.dot(a, b, preferred_element_type=jnp.float32).astype(jnp.bfloat16)  4.67 us
    unnamed x10, local copies, waits for them, and re-layouts  4.28 us
    pallas_call x1, Pallas kernels, in_exchange_order(): pl.pallas_call(order_kernel, out_shape=[jax.ShapeDtypeStruct((rows // 2,...  4.18 us
  transfers between devices with their start and end apart: 20, of which 13 were waited for; matrix products, arithmetic and copies ran while one was open for 6% of the time, Pallas kernels for 8%

profile of v1, /device:TPU:41, one launch (start us, length us, event | category | flops | bytes accessed | tf_op | source)
XLA Modules:
  0.0 96.6 jit_solution(7557579634837654849)
XLA Ops:
  0.7 0.1 stack.136.ids
  0.8 3.1 %copy-done.1 = bf16[1,896,4096]{2,1,0:T(8,128)(2,1)S(1)} copy-done((bf16[1,896,4096]{2,1,0:T(8,128)(2,1)S(1)}, bf16[1,896,4096]{2,1,0:T(8,128)(2,1)}, u32[]{:S(2)}) %copy-start.1) | copy-done | bytes 7340056
  3.9 1.2 %copy-done.2 = bf16[1,512,896]{2,1,0:T(8,128)(2,1)S(1)} copy-done((bf16[1,512,896]{2,1,0:T(8,128)(2,1)S(1)}, bf16[1,512,896]{2,1,0:T(8,128)(2,1)}, u32[]{:S(2)}) %copy-start.2) | copy-done | bytes 917528
  5.0 4.2 %shard_map.68 = (bf16[256,896]{1,0:T(8,128)(2,1)S(1)}, bf16[256,896]{1,0:T(8,128)(2,1)S(1)}, bf16[896,4096]{1,0:T(8,128)(2,1)S(1)}) custom-call(s32[32]{0:T(128)S(1)} %stack.136.ids, bf16[512,896]{1,0:T(8,128)(2,1)S(1)} %bitcast.43, bf16[896,4096]{1,0:T(8,128)(2,1)S(1)} %bitcast.42), custom_call_target="tpu_custom_call" | custom-call | bytes 16515072 | tf_op jit(solution)/shard_map/pallas_call | solution.py:88
  9.2 2.3 %convolution_convert_fusion = bf16[256,4096]{1,0:T(8,128)(2,1)S(1)} fusion(bf16[256,896]{1,0:T(8,128)(2,1)S(1)} %get-tuple-element.12, bf16[896,4096]{1,0:T(8,128)(2,1)S(1)} %get-tuple-element.11), kind=kOutput, calls=%fused_computation | convolution fusion | flops 1880096768 | bytes 9895936 | tf_op jit(solution)/shard_map/dot_general | solution.py:160
  11.6 0.2 fusion.8
  11.8 0.8 collective-permute-start.4
  12.6 0.1 collective-permute-start
  12.7 2.3 %convolution_convert_fusion.1 = bf16[256,4096]{1,0:T(8,128)(2,1)S(1)} fusion(bf16[256,896]{1,0:T(8,128)(2,1)S(1)} %get-tuple-element.10, bf16[896,4096]{1,0:T(8,128)(2,1)S(1)} %get-tuple-element.11), kind=kOutput, calls=%fused_computation.1 | convolution fusion | flops 1880096768 | bytes 9895936 | tf_op jit(solution)/shard_map/dot_general | solution.py:160
  15.0 0.0 copy-start.3
  15.0 0.0 collective-permute-done.4
  15.0 1.3 %collective-permute-done = bf16[128,4096]{1,0:T(8,128)(2,1)S(1)} collective-permute-done((bf16[128,4096]{1,0:T(8,128)(2,1)S(1)}, bf16[128,4096]{1,0:T(8,128)(2,1)S(1)}, u32[]{:S(2)}, u32[]{:S(2)}) %collective-permute-start) | collective-permute-done | bytes 1048608 | tf_op jit(solution)/shard_map/ppermute | solution.py:21
  16.3 0.8 add_convert_fusion.3
  17.1 0.0 copy-start.4
  17.2 2.6 %collective-permute-start.1 = (bf16[64,4096]{1,0:T(8,128)(2,1)S(1)}, bf16[64,4096]{1,0:T(8,128)(2,1)S(1)}, u32[]{:S(2)}, u32[]{:S(2)}) collective-permute-start(bf16[64,4096]{1,0:T(8,128)(2,1)S(1)} %get-tuple-element.19), channel_id=1, source_target_pairs={{0,4},{1,13},{2,6},{3,15},{4,0},{5,9},{6,2},{7,11},{8,12},{9,5},{1... | collective-permute-start | bytes 1572872 | tf_op jit(solution)/shard_map/ppermute | solution.py:21
  19.7 0.0 collective-permute-start.5
  19.7 6.8 %collective-permute-done.1 = bf16[64,4096]{1,0:T(8,128)(2,1)S(1)} collective-permute-done((bf16[64,4096]{1,0:T(8,128)(2,1)S(1)}, bf16[64,4096]{1,0:T(8,128)(2,1)S(1)}, u32[]{:S(2)}, u32[]{:S(2)}) %collective-permute-start.1) | collective-permute-done | bytes 524320 | tf_op jit(solution)/shard_map/ppermute | solution.py:21
  26.5 0.1 add_convert_fusion.7
  26.6 0.0 copy-start
  26.6 0.4 collective-permute-start.2
  27.0 6.5 %collective-permute-done.5 = bf16[64,4096]{1,0:T(8,128)(2,1)S(1)} collective-permute-done((bf16[64,4096]{1,0:T(8,128)(2,1)S(1)}, bf16[64,4096]{1,0:T(8,128)(2,1)S(1)}, u32[]{:S(2)}, u32[]{:S(2)}) %collective-permute-start.5) | collective-permute-done | bytes 524320 | tf_op jit(solution)/shard_map/ppermute | solution.py:21
  33.5 0.1 add_convert_fusion.5
  33.6 0.1 collective-permute-start.6
  33.7 0.0 collective-permute-done.2
  33.8 0.1 collective-permute-start.3
  33.9 6.3 %collective-permute-done.6 = bf16[32,4096]{1,0:T(8,128)(2,1)S(1)} collective-permute-done((bf16[32,4096]{1,0:T(8,128)(2,1)S(1)}, bf16[32,4096]{1,0:T(8,128)(2,1)S(1)}, u32[]{:S(2)}, u32[]{:S(2)}) %collective-permute-start.6) | collective-permute-done | bytes 262176 | tf_op jit(solution)/shard_map/ppermute | solution.py:21
  40.2 0.1 add_convert_fusion.8
  40.2 0.1 collective-permute-start.7
  40.4 0.1 fusion.7
  40.4 3.1 %collective-permute-start.9 = (bf16[16,4096]{1,0:T(8,128)(2,1)S(1)}, bf16[16,4096]{1,0:T(8,128)(2,1)S(1)}, u32[]{:S(2)}, u32[]{:S(2)}) collective-permute-start(bf16[16,4096]{1,0:T(8,128)(2,1)S(1)} %fusion.7), channel_id=1, source_target_pairs={{0,16},{16,32},{32,48},{48,0},{1,17},{17,33},{33,49},{49,1},{2,18}... | collective-permute-start | bytes 393224 | tf_op jit(solution)/shard_map/ppermute | solution.py:35
  43.5 0.6 collective-permute-done.7
  44.1 0.1 fusion.6
  44.2 3.1 %collective-permute-start.8 = (bf16[16,4096]{1,0:T(8,128)(2,1)S(1)}, bf16[16,4096]{1,0:T(8,128)(2,1)S(1)}, u32[]{:S(2)}, u32[]{:S(2)}) collective-permute-start(bf16[16,4096]{1,0:T(8,128)(2,1)S(1)} %fusion.6), channel_id=1, source_target_pairs={{0,16},{16,32},{32,48},{48,0},{1,17},{17,33},{33,49},{49,1},{2,18}... | collective-permute-start | bytes 393224 | tf_op jit(solution)/shard_map/ppermute | solution.py:35
  47.3 5.0 %collective-permute-done.9 = bf16[16,4096]{1,0:T(8,128)(2,1)S(1)} collective-permute-done((bf16[16,4096]{1,0:T(8,128)(2,1)S(1)}, bf16[16,4096]{1,0:T(8,128)(2,1)S(1)}, u32[]{:S(2)}, u32[]{:S(2)}) %collective-permute-start.9) | collective-permute-done | bytes 131104 | tf_op jit(solution)/shard_map/ppermute | solution.py:35
  52.3 0.1 fusion
  52.4 0.1 fusion.2
  52.5 0.3 collective-permute-start.14
  52.8 4.5 %collective-permute-done.8 = bf16[16,4096]{1,0:T(8,128)(2,1)S(1)} collective-permute-done((bf16[16,4096]{1,0:T(8,128)(2,1)S(1)}, bf16[16,4096]{1,0:T(8,128)(2,1)S(1)}, u32[]{:S(2)}, u32[]{:S(2)}) %collective-permute-start.8) | collective-permute-done | bytes 131104 | tf_op jit(solution)/shard_map/ppermute | solution.py:35
  57.3 0.1 fusion.3
  57.4 1.9 %collective-permute-done.14 = bf16[16,4096]{1,0:T(8,128)(2,1)S(1)} collective-permute-done((bf16[16,4096]{1,0:T(8,128)(2,1)S(1)}, bf16[16,4096]{1,0:T(8,128)(2,1)S(1)}, u32[]{:S(2)}, u32[]{:S(2)}) %collective-permute-start.14) | collective-permute-done | bytes 131104 | tf_op jit(solution)/shard_map/ppermute | solution.py:21
  59.3 2.8 %collective-permute-start.15 = (bf16[32,4096]{1,0:T(8,128)(2,1)S(1)}, bf16[32,4096]{1,0:T(8,128)(2,1)S(1)}, u32[]{:S(2)}, u32[]{:S(2)}) collective-permute-start(bf16[32,4096]{1,0:T(8,128)(2,1)S(1)} %pad_maximum_fusion.3), channel_id=1, source_target_pairs={{0,12},{1,5},{2,14},{3,7},{4,8},{5,1},{6,10},{7,3},{8,4},{9,13},{1... | collective-permute-start | bytes 786440 | tf_op jit(solution)/shard_map/ppermute | solution.py:21
  62.1 0.1 fusion.5
  62.2 0.1 collective-permute-start.10
  62.3 3.9 %collective-permute-done.15 = bf16[32,4096]{1,0:T(8,128)(2,1)S(1)} collective-permute-done((bf16[32,4096]{1,0:T(8,128)(2,1)S(1)}, bf16[32,4096]{1,0:T(8,128)(2,1)S(1)}, u32[]{:S(2)}, u32[]{:S(2)}) %collective-permute-start.15) | collective-permute-done | bytes 262176 | tf_op jit(solution)/shard_map/ppermute | solution.py:21
  66.2 0.8 pad_maximum_fusion.1.refs_0_
  67.0 0.0 collective-permute-start.16
  67.0 0.7 collective-permute-done.10
  67.8 0.8 collective-permute-start.11
  68.6 2.7 %collective-permute-start.17 = (bf16[64,4096]{1,0:T(8,128)(2,1)}, bf16[64,4096]{1,0:T(8,128)(2,1)}, u32[]{:S(2)}, u32[]{:S(2)}) collective-permute-start(bf16[64,4096]{1,0:T(8,128)(2,1)} %pad_maximum_fusion.1.refs_0_), channel_id=1, source_target_pairs={{0,1},{1,0},{2,3},{3,2},{4,5},{5,4},{6,7},{7,6},{8,9},{9,8},{10,11... | collective-permute-start | bytes 1572872 | tf_op jit(solution)/shard_map/ppermute | solution.py:21
  71.3 7.7 %collective-permute-done.16.refs_1_ = bf16[64,4096]{1,0:T(8,128)(2,1)} collective-permute-done((bf16[64,4096]{1,0:T(8,128)(2,1)}, bf16[64,4096]{1,0:T(8,128)(2,1)}, u32[]{:S(2)}, u32[]{:S(2)}) %collective-permute-start.16) | collective-permute-done | bytes 524320 | tf_op jit(solution)/shard_map/ppermute | solution.py:21
  79.0 0.5 collective-permute-start.18
  79.5 0.8 pad_maximum_fusion.refs_0_
  80.4 0.5 collective-permute-start.13
  80.8 1.5 %collective-permute-start.12 = (bf16[64,4096]{1,0:T(8,128)(2,1)}, bf16[64,4096]{1,0:T(8,128)(2,1)}, u32[]{:S(2)}, u32[]{:S(2)}) collective-permute-start(bf16[64,4096]{1,0:T(8,128)(2,1)} %pad_maximum_fusion.refs_0_), channel_id=1, source_target_pairs={{0,4},{1,13},{2,6},{3,15},{4,0},{5,9},{6,2},{7,11},{8,12},{9,5},{1... | collective-permute-start | bytes 1572872 | tf_op jit(solution)/shard_map/ppermute | solution.py:21
  82.3 0.1 stack.137.ids
  82.4 0.0 collective-permute-done.17.refs_2_
  82.5 4.1 %shard_map.69.refs_3_ = bf16[512,384]{1,0:T(8,128)(2,1)S(1)} custom-call(s32[32]{0:T(128)S(1)} %stack.137.ids, bf16[64,4096]{1,0:T(8,128)(2,1)} %pad_maximum_fusion.1.refs_0_, bf16[64,4096]{1,0:T(8,128)(2,1)} %collective-permute-done.16.refs_1_, bf16[64,4096]{1,0:T(8,128)(2,1)} %collective-permute-done.17.refs_2_, ...), custom_call_target="tpu_custom_call" | custom-call | flops 805306368 | bytes 5636096 | tf_op jit(solution)/shard_map/pallas_call | solution.py:138
  86.6 0.0 collective-permute-done.13.refs_1_
  86.6 3.5 %shard_map.70.refs_3_ = bf16[512,384]{1,0:T(8,128)(2,1)S(1)} custom-call(s32[32]{0:T(128)S(1)} %stack.137.ids, bf16[64,4096]{1,0:T(8,128)(2,1)} %pad_maximum_fusion.refs_0_, bf16[64,4096]{1,0:T(8,128)(2,1)} %collective-permute-done.13.refs_1_, bf16[4096,384]{1,0:T(8,128)(2,1)S(1)} %bitcast.40, bf16[512,384]{1,0:T(8,128)(2,1)S(1)} %shard_map.69.refs_3_), custom_call_target="tpu_custom_call" | custom-call | flops 402653184 | bytes 4587520 | tf_op jit(solution)/shard_map/pallas_call | solution.py:138
  90.1 0.3 collective-permute-done.12.refs_0_
  90.4 0.0 collective-permute-start.19
  90.4 0.7 maximum_bitcast_fusion
  91.1 1.4 %collective-permute-done.19.refs_1_ = bf16[64,4096]{1,0:T(8,128)(2,1)S(1)} collective-permute-done((bf16[64,4096]{1,0:T(8,128)(2,1)}, bf16[64,4096]{1,0:T(8,128)(2,1)S(1)}, u32[]{:S(2)}, u32[]{:S(2)}) %collective-permute-start.19) | collective-permute-done | bytes 524320 | tf_op jit(solution)/shard_map/ppermute | solution.py:21
  92.5 4.1 %shard_map.71 = bf16[512,384]{1,0:T(8,128)(2,1)} custom-call(s32[32]{0:T(128)S(1)} %stack.137.ids, bf16[64,4096]{1,0:T(8,128)(2,1)} %collective-permute-done.12.refs_0_, bf16[64,4096]{1,0:T(8,128)(2,1)S(1)} %collective-permute-done.19.refs_1_, bf16[4096,384]{1,0:T(8,128)(2,1)S(1)} %bitcast.41, bf16[512,384]{1,0:T(8,128)(2,1)S(1)} %shard_map.70.refs_3_), custom_call_target="tpu_custom_call" | custom-call | flops 402653184 | bytes 4587520 | tf_op jit(solution)/shard_map/pallas_call | solution.py:138
  (13 shorter events, 0.1 us)
Async XLA Ops:
  0.8 3.1 %copy-start.1 = (bf16[1,896,4096]{2,1,0:T(8,128)(2,1)S(1)}, bf16[1,896,4096]{2,1,0:T(8,128)(2,1)}, u32[]{:S(2)}) copy-start(bf16[1,896,4096]{2,1,0:T(8,128)(2,1)} %param.8) | copy-start | bytes 22020100
  3.9 1.2 %copy-start.2 = (bf16[1,512,896]{2,1,0:T(8,128)(2,1)S(1)}, bf16[1,512,896]{2,1,0:T(8,128)(2,1)}, u32[]{:S(2)}) copy-start(bf16[1,512,896]{2,1,0:T(8,128)(2,1)} %param.5) | copy-start | bytes 2752516
  11.8 3.2 %collective-permute-start.4 = (bf16[128,4096]{1,0:T(8,128)(2,1)S(1)}, bf16[128,4096]{1,0:T(8,128)(2,1)S(1)}, u32[]{:S(2)}, u32[]{:S(2)}) collective-permute-start(bf16[128,4096]{1,0:T(8,128)(2,1)S(1)} %get-tuple-element.25), channel_id=1, source_target_pairs={{0,1},{1,0},{2,3},{3,2},{4,5},{5,4},{6,7},{7,6},{8,9},{9,8},{10,11... | collective-permute-start | bytes 3145736 | tf_op jit(solution)/shard_map/ppermute | solution.py:21
  12.6 3.8 %collective-permute-start = (bf16[128,4096]{1,0:T(8,128)(2,1)S(1)}, bf16[128,4096]{1,0:T(8,128)(2,1)S(1)}, u32[]{:S(2)}, u32[]{:S(2)}) collective-permute-start(bf16[128,4096]{1,0:T(8,128)(2,1)S(1)} %get-tuple-element.24), channel_id=1, source_target_pairs={{0,1},{1,0},{2,3},{3,2},{4,5},{5,4},{6,7},{7,6},{8,9},{9,8},{10,11... | collective-permute-start | bytes 3145736 | tf_op jit(solution)/shard_map/ppermute | solution.py:21
  15.0 25.3 %copy-start.3 = (bf16[1,32,4096]{2,1,0:T(8,128)(2,1)S(1)}, bf16[1,32,4096]{2,1,0:T(8,128)(2,1)}, u32[]{:S(2)}) copy-start(bf16[1,32,4096]{2,1,0:T(8,128)(2,1)} %param.6) | copy-start | bytes 786436
  17.1 35.3 %copy-start.4 = (f32[1,4096]{1,0:T(1,128)S(1)}, f32[1,4096]{1,0:T(1,128)}, u32[]{:S(2)}) copy-start(f32[1,4096]{1,0:T(1,128)} %param.7) | copy-start | bytes 49156
  17.2 9.3 %collective-permute-start.1 = (bf16[64,4096]{1,0:T(8,128)(2,1)S(1)}, bf16[64,4096]{1,0:T(8,128)(2,1)S(1)}, u32[]{:S(2)}, u32[]{:S(2)}) collective-permute-start(bf16[64,4096]{1,0:T(8,128)(2,1)S(1)} %get-tuple-element.19), channel_id=1, source_target_pairs={{0,4},{1,13},{2,6},{3,15},{4,0},{5,9},{6,2},{7,11},{8,12},{9,5},{1... | collective-permute-start | bytes 1572872 | tf_op jit(solution)/shard_map/ppermute | solution.py:21
  19.7 13.8 %collective-permute-start.5 = (bf16[64,4096]{1,0:T(8,128)(2,1)S(1)}, bf16[64,4096]{1,0:T(8,128)(2,1)S(1)}, u32[]{:S(2)}, u32[]{:S(2)}) collective-permute-start(bf16[64,4096]{1,0:T(8,128)(2,1)S(1)} %get-tuple-element.22), channel_id=1, source_target_pairs={{0,2},{1,3},{2,0},{3,1},{4,6},{5,7},{6,4},{7,5},{8,10},{9,11},{10,... | collective-permute-start | bytes 1572872 | tf_op jit(solution)/shard_map/ppermute | solution.py:21
  26.6 55.8 %copy-start = (bf16[1,4096,384]{2,1,0:T(8,128)(2,1)S(1)}, bf16[1,4096,384]{2,1,0:T(8,128)(2,1)}, u32[]{:S(2)}) copy-start(bf16[1,4096,384]{2,1,0:T(8,128)(2,1)} %param.9) | copy-start | bytes 9437188
  26.6 7.1 %collective-permute-start.2 = (bf16[32,4096]{1,0:T(8,128)(2,1)S(1)}, bf16[32,4096]{1,0:T(8,128)(2,1)S(1)}, u32[]{:S(2)}, u32[]{:S(2)}) collective-permute-start(bf16[32,4096]{1,0:T(8,128)(2,1)S(1)} %get-tuple-element.27), channel_id=1, source_target_pairs={{0,12},{1,5},{2,14},{3,7},{4,8},{5,1},{6,10},{7,3},{8,4},{9,13},{1... | collective-permute-start | bytes 786440 | tf_op jit(solution)/shard_map/ppermute | solution.py:21
  33.6 6.5 %collective-permute-start.6 = (bf16[32,4096]{1,0:T(8,128)(2,1)S(1)}, bf16[32,4096]{1,0:T(8,128)(2,1)S(1)}, u32[]{:S(2)}, u32[]{:S(2)}) collective-permute-start(bf16[32,4096]{1,0:T(8,128)(2,1)S(1)} %get-tuple-element.29), channel_id=1, source_target_pairs={{0,4},{1,13},{2,6},{3,15},{4,0},{5,9},{6,2},{7,11},{8,12},{9,5},{1... | collective-permute-start | bytes 786440 | tf_op jit(solution)/shard_map/ppermute | solution.py:21
  33.8 6.5 %collective-permute-start.3 = (bf16[16,4096]{1,0:T(8,128)(2,1)S(1)}, bf16[16,4096]{1,0:T(8,128)(2,1)S(1)}, u32[]{:S(2)}, u32[]{:S(2)}) collective-permute-start(bf16[16,4096]{1,0:T(8,128)(2,1)S(1)} %add_convert_fusion.10), channel_id=1, source_target_pairs={{0,2},{1,3},{2,0},{3,1},{4,6},{5,7},{6,4},{7,5},{8,10},{9,11},{10,... | collective-permute-start | bytes 393224 | tf_op jit(solution)/shard_map/ppermute | solution.py:21
  40.2 3.9 %collective-permute-start.7 = (bf16[16,4096]{1,0:T(8,128)(2,1)S(1)}, bf16[16,4096]{1,0:T(8,128)(2,1)S(1)}, u32[]{:S(2)}, u32[]{:S(2)}) collective-permute-start(bf16[16,4096]{1,0:T(8,128)(2,1)S(1)} %get-tuple-element.30), channel_id=1, source_target_pairs={{0,12},{1,5},{2,14},{3,7},{4,8},{5,1},{6,10},{7,3},{8,4},{9,13},{1... | collective-permute-start | bytes 393224 | tf_op jit(solution)/shard_map/ppermute | solution.py:21
  40.4 11.8 %collective-permute-start.9 = (bf16[16,4096]{1,0:T(8,128)(2,1)S(1)}, bf16[16,4096]{1,0:T(8,128)(2,1)S(1)}, u32[]{:S(2)}, u32[]{:S(2)}) collective-permute-start(bf16[16,4096]{1,0:T(8,128)(2,1)S(1)} %fusion.7), channel_id=1, source_target_pairs={{0,16},{16,32},{32,48},{48,0},{1,17},{17,33},{33,49},{49,1},{2,18}... | collective-permute-start | bytes 393224 | tf_op jit(solution)/shard_map/ppermute | solution.py:35
  44.2 13.1 %collective-permute-start.8 = (bf16[16,4096]{1,0:T(8,128)(2,1)S(1)}, bf16[16,4096]{1,0:T(8,128)(2,1)S(1)}, u32[]{:S(2)}, u32[]{:S(2)}) collective-permute-start(bf16[16,4096]{1,0:T(8,128)(2,1)S(1)} %fusion.6), channel_id=1, source_target_pairs={{0,16},{16,32},{32,48},{48,0},{1,17},{17,33},{33,49},{49,1},{2,18}... | collective-permute-start | bytes 393224 | tf_op jit(solution)/shard_map/ppermute | solution.py:35
  52.5 6.8 %collective-permute-start.14 = (bf16[16,4096]{1,0:T(8,128)(2,1)S(1)}, bf16[16,4096]{1,0:T(8,128)(2,1)S(1)}, u32[]{:S(2)}, u32[]{:S(2)}) collective-permute-start(bf16[16,4096]{1,0:T(8,128)(2,1)S(1)} %fusion.2), channel_id=1, source_target_pairs={{0,2},{1,3},{2,0},{3,1},{4,6},{5,7},{6,4},{7,5},{8,10},{9,11},{10,... | collective-permute-start | bytes 393224 | tf_op jit(solution)/shard_map/ppermute | solution.py:21
  59.3 6.9 %collective-permute-start.15 = (bf16[32,4096]{1,0:T(8,128)(2,1)S(1)}, bf16[32,4096]{1,0:T(8,128)(2,1)S(1)}, u32[]{:S(2)}, u32[]{:S(2)}) collective-permute-start(bf16[32,4096]{1,0:T(8,128)(2,1)S(1)} %pad_maximum_fusion.3), channel_id=1, source_target_pairs={{0,12},{1,5},{2,14},{3,7},{4,8},{5,1},{6,10},{7,3},{8,4},{9,13},{1... | collective-permute-start | bytes 786440 | tf_op jit(solution)/shard_map/ppermute | solution.py:21
  62.2 5.5 %collective-permute-start.10 = (bf16[16,4096]{1,0:T(8,128)(2,1)S(1)}, bf16[16,4096]{1,0:T(8,128)(2,1)S(1)}, u32[]{:S(2)}, u32[]{:S(2)}) collective-permute-start(bf16[16,4096]{1,0:T(8,128)(2,1)S(1)} %fusion.5), channel_id=1, source_target_pairs={{0,2},{1,3},{2,0},{3,1},{4,6},{5,7},{6,4},{7,5},{8,10},{9,11},{10,... | collective-permute-start | bytes 393224 | tf_op jit(solution)/shard_map/ppermute | solution.py:21
  67.0 11.9 %collective-permute-start.16 = (bf16[64,4096]{1,0:T(8,128)(2,1)}, bf16[64,4096]{1,0:T(8,128)(2,1)}, u32[]{:S(2)}, u32[]{:S(2)}) collective-permute-start(bf16[64,4096]{1,0:T(8,128)(2,1)} %pad_maximum_fusion.1.refs_0_), channel_id=1, source_target_pairs={{0,4},{1,13},{2,6},{3,15},{4,0},{5,9},{6,2},{7,11},{8,12},{9,5},{1... | collective-permute-start | bytes 1572872 | tf_op jit(solution)/shard_map/ppermute | solution.py:21
  67.8 11.7 %collective-permute-start.11 = (bf16[32,4096]{1,0:T(8,128)(2,1)S(1)}, bf16[32,4096]{1,0:T(8,128)(2,1)S(1)}, u32[]{:S(2)}, u32[]{:S(2)}) collective-permute-start(bf16[32,4096]{1,0:T(8,128)(2,1)S(1)} %pad_maximum_fusion.2), channel_id=1, source_target_pairs={{0,12},{1,5},{2,14},{3,7},{4,8},{5,1},{6,10},{7,3},{8,4},{9,13},{1... | collective-permute-start | bytes 786440 | tf_op jit(solution)/shard_map/ppermute | solution.py:21
  68.6 13.8 %collective-permute-start.17 = (bf16[64,4096]{1,0:T(8,128)(2,1)}, bf16[64,4096]{1,0:T(8,128)(2,1)}, u32[]{:S(2)}, u32[]{:S(2)}) collective-permute-start(bf16[64,4096]{1,0:T(8,128)(2,1)} %pad_maximum_fusion.1.refs_0_), channel_id=1, source_target_pairs={{0,1},{1,0},{2,3},{3,2},{4,5},{5,4},{6,7},{7,6},{8,9},{9,8},{10,11... | collective-permute-start | bytes 1572872 | tf_op jit(solution)/shard_map/ppermute | solution.py:21
  79.0 3.5 %collective-permute-start.18 = (bf16[64,4096]{1,0:T(8,128)(2,1)}, bf16[64,4096]{1,0:T(8,128)(2,1)}, u32[]{:S(2)}, u32[]{:S(2)}) collective-permute-start(bf16[64,4096]{1,0:T(8,128)(2,1)} %collective-permute-done.16.refs_1_), channel_id=1, source_target_pairs={{0,1},{1,0},{2,3},{3,2},{4,5},{5,4},{6,7},{7,6},{8,9},{9,8},{10,11... | collective-permute-start | bytes 1572872 | tf_op jit(solution)/shard_map/ppermute | solution.py:21
  80.4 6.2 %collective-permute-start.13 = (bf16[64,4096]{1,0:T(8,128)(2,1)}, bf16[64,4096]{1,0:T(8,128)(2,1)}, u32[]{:S(2)}, u32[]{:S(2)}) collective-permute-start(bf16[64,4096]{1,0:T(8,128)(2,1)} %pad_maximum_fusion.refs_0_), channel_id=1, source_target_pairs={{0,1},{1,0},{2,3},{3,2},{4,5},{5,4},{6,7},{7,6},{8,9},{9,8},{10,11... | collective-permute-start | bytes 1572872 | tf_op jit(solution)/shard_map/ppermute | solution.py:21
  80.8 9.6 %collective-permute-start.12 = (bf16[64,4096]{1,0:T(8,128)(2,1)}, bf16[64,4096]{1,0:T(8,128)(2,1)}, u32[]{:S(2)}, u32[]{:S(2)}) collective-permute-start(bf16[64,4096]{1,0:T(8,128)(2,1)} %pad_maximum_fusion.refs_0_), channel_id=1, source_target_pairs={{0,4},{1,13},{2,6},{3,15},{4,0},{5,9},{6,2},{7,11},{8,12},{9,5},{1... | collective-permute-start | bytes 1572872 | tf_op jit(solution)/shard_map/ppermute | solution.py:21
  90.4 2.1 %collective-permute-start.19 = (bf16[64,4096]{1,0:T(8,128)(2,1)}, bf16[64,4096]{1,0:T(8,128)(2,1)S(1)}, u32[]{:S(2)}, u32[]{:S(2)}) collective-permute-start(bf16[64,4096]{1,0:T(8,128)(2,1)} %collective-permute-done.12.refs_0_), channel_id=1, source_target_pairs={{0,1},{1,0},{2,3},{3,2},{4,5},{5,4},{6,7},{7,6},{8,9},{9,8},{10,11... | collective-permute-start | bytes 1572872 | tf_op jit(solution)/shard_map/ppermute | solution.py:21

commit v2 on v0

v2 whole, which is shorter than its diff:
```python
import functools
import itertools

import jax
import jax.numpy as jnp
from jax import lax
from jax.experimental import pallas as pl
from jax.experimental.pallas import tpu as pltpu
from jax.sharding import Mesh, PartitionSpec as P

AXES = ("x", "z", "core")
SIZES = (4, 2, 2)
TRADES = {
    "o": ((0, 0), 0, 0),
    "a": ((1, 3), 0, 0),
    "b": ((3, 1), 0, 0),
    "z": ((0, 0), 1, 0),
    "ab": ((2, 2), 0, 0),
    "az": ((1, 3), 1, 0),
    "bz": ((3, 1), 1, 0),
    "abz": ((2, 2), 1, 0),
    "core": ((0, 0), 0, 1),
}
FIRST = ("abz", "bz", "az", "a")
SECOND = ("ab", "b", "z", "o")
GATHERED = ("o", "ab", "a", "b", "z", "az", "abz", "bz")


def trade(value, name):
    x_mask, z_mask, core_mask = TRADES[name]
    pairs = []
    for x, z, c in itertools.product(*map(range, SIZES)):
        to = ((x ^ x_mask[c]) * 2 + (z ^ z_mask)) * 2 + (c ^ core_mask)
        pairs.append(((x * 2 + z) * 2 + c, to))
    return lax.ppermute(value, AXES, pairs)


def next_section(value):
    count = lax.axis_size("pipe")
    return lax.ppermute(value, "pipe", [(s, (s + 1) % count) for s in range(count)])


def after(value, *others):
    return lax.optimization_barrier((value,) + others)[0]


def normalize(values, gain_row):
    wide = values.astype(jnp.float32)
    scaler = lax.rsqrt(jnp.mean(wide * wide, axis=-1, keepdims=True) + 1e-05)
    return (wide * scaler * gain_row).astype(jnp.bfloat16)


def block_ids(names):
    x, z, core = (lax.axis_index(a) for a in AXES)
    ids = []
    for c in (core, 1 - core):
        for name in names:
            (m0, m1), zm, _ = TRADES[name]
            m = m0 + (m1 - m0) * c
            ids.append(((x ^ m) * 2 + (z ^ zm)) * 2 + c)
    return jnp.stack(ids).astype(jnp.int32)


def pick_kernel(ids, hid_ref, mine_ref, theirs_ref):
    rows = hid_ref.shape[0] // 16
    for i in range(16):
        start = pl.multiple_of(ids[i] * rows, rows)
        out = (mine_ref, theirs_ref)[i // 8]
        out[i % 8 * rows : (i % 8 + 1) * rows, :] = hid_ref[pl.ds(start, rows), :]


def pick(ids, hid):
    rows, depth = hid.shape
    return pl.pallas_call(
        pick_kernel,
        out_shape=[jax.ShapeDtypeStruct((rows // 2, depth), jnp.bfloat16)] * 2,
        in_specs=[pl.BlockSpec(memory_space=pltpu.SMEM), pl.BlockSpec(memory_space=pltpu.VMEM)],
        out_specs=[pl.BlockSpec(memory_space=pltpu.VMEM)] * 2,
        compiler_params=pltpu.CompilerParams(vmem_limit_bytes=4 << 20),
        cost_estimate=pl.CostEstimate(flops=0, bytes_accessed=4 * rows * depth, transcendentals=0),
    )(ids, hid)


def product(parts, w_ref):
    deep = w_ref.shape[0] // 4
    total = None
    for i in range(4):
        at = slice(i * deep, (i + 1) * deep)
        lhs = jnp.concatenate([p[:, at] for p in parts], axis=0)
        term = jnp.dot(lhs, w_ref[at, :], preferred_element_type=jnp.float32)
        total = term if total is None else total + term
    return total.astype(jnp.bfloat16)


def project_kernel(places, ids, w_ref, *refs):
    out_ref, ready_ref, rows_ref, sem = refs[-4:]
    parts = refs[:-4] if len(places) == len(refs) - 4 else refs[1:-4]
    rows = rows_ref.shape[0] // len(places)
    rows_ref[...] = product(parts, w_ref)
    copies = []
    for i, at in enumerate(places):
        start = pl.multiple_of(ids[at] * rows, rows)
        copies.append(
            pltpu.make_async_copy(
                rows_ref.at[pl.ds(i * rows, rows), :], out_ref.at[pl.ds(start, rows), :], sem.at[i]
            )
        )
    for c in copies:
        c.start()
    ready_ref[...] = jnp.zeros_like(ready_ref)
    for c in copies:
        c.wait()


def project(pieces, places, ids, w, before=None, weight=1):
    rows = pieces[0].shape[0]
    depth, width = w.shape
    n = len(pieces)
    extra = [] if before is None else [before]
    vmem = pl.BlockSpec(memory_space=pltpu.VMEM)
    anywhere = pl.BlockSpec(memory_space=pl.ANY)
    return pl.pallas_call(
        functools.partial(project_kernel, places),
        out_shape=[
            jax.ShapeDtypeStruct((16 * rows, width), jnp.bfloat16),
            jax.ShapeDtypeStruct((8, 128), jnp.float32),
        ],
        in_specs=[pl.BlockSpec(memory_space=pltpu.SMEM), vmem] + [anywhere] * len(extra) + [vmem] * n,
        out_specs=[anywhere, vmem],
        scratch_shapes=[
            pltpu.VMEM((n * rows, width), jnp.bfloat16),
            pltpu.SemaphoreType.DMA((n,)),
        ],
        input_output_aliases={2: 0} if extra else {},
        compiler_params=pltpu.CompilerParams(vmem_limit_bytes=16 << 20),
        cost_estimate=pl.CostEstimate(
            flops=weight * 2 * n * rows * depth * width,
            bytes_accessed=2 * (n * rows * depth + depth * width + n * rows * width),
            transcendentals=0,
        ),
    )(ids, w, *extra, *pieces)


def dot_bf16(a, b):
    return jnp.dot(a, b, preferred_element_type=jnp.float32).astype(jnp.bfloat16)


def add(*terms):
    return sum(t.astype(jnp.float32) for t in terms)


def shards(hidden, residual, norm_gain, down_weight, qkv_weight):
    resid = residual[0]
    gain = norm_gain[0]
    qkv = qkv_weight[0]
    down = down_weight[0]
    rows = resid.shape[0]
    half = 4 * rows
    mine, theirs = pick(block_ids(FIRST + SECOND), hidden[0])
    out_ids = block_ids(GATHERED)

    sent = lax.optimization_barrier(dot_bf16(theirs, down))
    first, second = (lax.optimization_barrier(s) for s in (sent[:half], sent[half:]))
    kept = lax.optimization_barrier(dot_bf16(mine, down))
    got = trade(first, "core")

    def both(lo, hi):
        at = slice(lo * rows, hi * rows)
        return lax.optimization_barrier(add(kept[at], got[at]).astype(jnp.bfloat16))

    abz, az_a, bz = both(0, 1), both(2, 4), both(1, 2)
    for_ab = trade(abz, "z")
    for_z_o = trade(az_a, "a")
    for_b = trade(bz, "z")
    got = trade(second, "core")
    own = [(kept[half + i * rows : half + (i + 1) * rows], got[i * rows : (i + 1) * rows]) for i in range(4)]
    ab = lax.optimization_barrier(add(*own[0], for_ab).astype(jnp.bfloat16))
    last_ab = trade(ab, "ab")
    z = lax.optimization_barrier(add(*own[2], after(for_z_o, ab)[:rows]).astype(jnp.bfloat16))
    last_z = trade(z, "z")
    b = lax.optimization_barrier(add(*own[1], after(for_b, z)).astype(jnp.bfloat16))
    last_b = trade(b, "b")
    out = add(resid, *own[3], for_z_o[rows:], last_ab, last_z, last_b).astype(jnp.bfloat16)
    out = lax.optimization_barrier(out)

    normed = lax.optimization_barrier(normalize(next_section(out), gain))
    ab = trade(normed, "ab")
    z = trade(normed, "z")
    b = trade(normed, "b")
    a = trade(normed, "a")
    az = trade(z, "a")
    abz = trade(z, "ab")
    bz = trade(b, "z")
    near = [after(t, ab, b, a) for t in (normed, ab, a, b, z)]
    near_swap = [trade(t, "core") for t in near]
    near_places = (0, 1, 2, 3, 4, 8, 9, 10, 11, 12)
    rows_near, ready = project(near + near_swap, near_places, out_ids, qkv, weight=20)
    late = [after(t, ready) for t in (az, bz, abz)]
    late_swap = [trade(t, "core") for t in late]
    late_places = (5, 7, 6, 13, 15, 14)
    proj, _ = project(late + late_swap, late_places, out_ids, qkv, before=rows_near)
    return (out[None], proj[None])


def solution(mesh):
    fine = Mesh(mesh.devices.reshape((4, 4) + SIZES), ("dp", "pipe") + AXES)
    return jax.shard_map(
        shards,
        mesh=fine,
        in_specs=(
            P("pipe", "dp", AXES),
            P("pipe", ("dp",) + AXES, None),
            P("pipe", None),
            P("pipe", AXES, None),
            P("pipe", None, AXES),
        ),
        out_specs=(P("pipe", ("dp",) + AXES, None), P("pipe", "dp", AXES)),
        check_vma=False,
    )
```

time: 410 us -> 86.4 us (0.21)
  waiting for transfers between devices: 365 us -> 40.9 us
  starting transfers between devices: 2.34 us -> 25.7 us
  between operations: 14.1 us -> 1.02 us
  other arithmetic: 10.3 us -> 1.09 us
  Pallas kernels: 0 us -> 7.9 us
  matrix products: 15.3 us -> 8.06 us
    ppermute x1 -> x24, waiting for transfers between devices: 181 us -> 40.9 us  [the longest x23 27.9 us: trade(): return lax.ppermute(value, AXES, pairs)]
    psum x1 -> x0, waiting for transfers between devices: 137 us -> none  [shards(): lax.psum(jnp.dot(hidden_rows, down_local, preferred_element_type=jnp.floa...]
    all_gather x1 -> x0, waiting for transfers between devices: 46.5 us -> none  [shards(): resid_full = lax.all_gather(resid_rows, 'tensor', axis=0, tiled=True)]
    ppermute x1 -> x24, starting transfers between devices: 2.27 us -> 25.7 us  [the longest x23 22.6 us: trade(): return lax.ppermute(value, AXES, pairs)]
    pallas_call x0 -> x3, Pallas kernels: none -> 7.9 us  [the longest x2 7.28 us: project(): pl.pallas_call(functools.partial(project_kernel, places), out_shape=[jax....]
    dot_general x2, matrix products: 15.3 us -> 8.06 us  [dot_bf16(): jnp.dot(a, b, preferred_element_type=jnp.float32).astype(jnp.bfloat16)]
    convert_element_type x1 -> x7, other arithmetic: 7.18 us -> 0.91 us  [the longest x2 0.25 us: both(): return lax.optimization_barrier(add(kept[at], got[at]).astype(jnp.bfloat16))]
  transfers between devices with their start and end apart: 3 -> 24, of which waited for: 3 -> 11; matrix products, arithmetic and copies ran while one was open for 0% -> 3% of each run, Pallas kernels for 0% -> 5%
where the time goes in v2:
time: 86.4 us; the launch traced here: 86.2 us
  waiting for transfers between devices  40.9 us (47%)
  starting transfers between devices  25.7 us (30%)
  matrix products  8.06 us (9%)
  Pallas kernels  7.9 us (9%)
  local copies, waits for them, and re-layouts  1.61 us (2%)
  other arithmetic  1.09 us (1%)
  between operations  1.02 us (1%)
    ppermute x23, waiting for transfers between devices, trade(): return lax.ppermute(value, AXES, pairs)  27.9 us
    ppermute x23, starting transfers between devices, trade(): return lax.ppermute(value, AXES, pairs)  22.6 us
    ppermute x1, waiting for transfers between devices, next_section(): lax.ppermute(value, 'pipe', [(s, (s + 1) % count) for s in range(count)])  13 us
    dot_general x2, matrix products, dot_bf16(): jnp.dot(a, b, preferred_element_type=jnp.float32).astype(jnp.bfloat16)  8.06 us
    pallas_call x2, Pallas kernels, project(): pl.pallas_call(functools.partial(project_kernel, places), out_shape=[jax....  7.28 us
    ppermute x1, starting transfers between devices, next_section(): lax.ppermute(value, 'pipe', [(s, (s + 1) % count) for s in range(count)])  3.07 us
  transfers between devices with their start and end apart: 24, of which 11 were waited for; matrix products, arithmetic and copies ran while one was open for 3% of the time, Pallas kernels for 5%

profile of v2, /device:TPU:41, one launch (start us, length us, event | category | flops | bytes accessed | tf_op | source)
XLA Modules:
  0.0 86.2 jit_solution(13694433879035557577)
XLA Ops:
  0.7 0.1 stack.86.ids
  0.8 0.0 copy-start.1
  0.8 1.2 %copy-done.1 = bf16[1,512,896]{2,1,0:T(8,128)(2,1)S(1)} copy-done((bf16[1,512,896]{2,1,0:T(8,128)(2,1)S(1)}, bf16[1,512,896]{2,1,0:T(8,128)(2,1)}, u32[]{:S(2)}) %copy-start.1) | copy-done | bytes 917528
  2.0 0.6 shard_map.68
  2.6 0.0 slice-start.1
  2.6 5.7 %fusion.7 = bf16[256,4096]{1,0:T(8,128)(2,1)S(1)} fusion(bf16[256,896]{1,0:T(8,128)(2,1)S(1)} %get-tuple-element.18, bf16[1,896,4096]{2,1,0:T(8,128)(2,1)} %param.8), kind=kOutput, calls=%fused_computation.5 | convolution fusion | flops 1880096768 | bytes 9895936 | tf_op jit(solution)/shard_map/dot_general | solution.py:145
  8.3 0.2 fusion.19
  8.5 0.8 collective-permute-start.1
  9.3 0.1 collective-permute-start
  9.4 2.3 %fusion.4 = bf16[256,4096]{1,0:T(8,128)(2,1)S(1)} fusion(bf16[256,896]{1,0:T(8,128)(2,1)S(1)} %get-tuple-element.17, bf16[1,896,4096]{2,1,0:T(8,128)(2,1)S(1)} %bitcast.42), kind=kOutput, calls=%fused_computation.4 | convolution fusion | flops 1880096768 | bytes 9895936 | tf_op jit(solution)/shard_map/dot_general | solution.py:145
  11.8 0.0 collective-permute-done.1
  11.8 0.1 add_convert_fusion.5
  11.9 0.0 copy-start.2
  11.9 0.1 collective-permute-start.3
  12.0 0.1 add_convert_fusion
  12.1 2.6 %collective-permute-start.2 = (bf16[64,4096]{1,0:T(8,128)(2,1)S(1)}, bf16[64,4096]{1,0:T(8,128)(2,1)S(1)}, u32[]{:S(2)}, u32[]{:S(2)}) collective-permute-start(bf16[64,4096]{1,0:T(8,128)(2,1)S(1)} %add_convert_fusion), channel_id=1, source_target_pairs={{0,4},{1,13},{2,6},{3,15},{4,0},{5,9},{6,2},{7,11},{8,12},{9,5},{1... | collective-permute-start | bytes 1572872 | tf_op jit(solution)/shard_map/ppermute | solution.py:35
  14.7 1.4 %collective-permute-start.6 = (bf16[32,4096]{1,0:T(8,128)(2,1)S(1)}, bf16[32,4096]{1,0:T(8,128)(2,1)S(1)}, u32[]{:S(2)}, u32[]{:S(2)}) collective-permute-start(bf16[32,4096]{1,0:T(8,128)(2,1)S(1)} %get-tuple-element.33), channel_id=1, source_target_pairs={{0,2},{1,3},{2,0},{3,1},{4,6},{5,7},{6,4},{7,5},{8,10},{9,11},{10,... | collective-permute-start | bytes 786440 | tf_op jit(solution)/shard_map/ppermute | solution.py:35
  16.2 0.0 collective-permute-done
  16.2 3.3 %collective-permute-done.3 = bf16[32,4096]{1,0:T(8,128)(2,1)S(1)} collective-permute-done((bf16[32,4096]{1,0:T(8,128)(2,1)S(1)}, bf16[32,4096]{1,0:T(8,128)(2,1)S(1)}, u32[]{:S(2)}, u32[]{:S(2)}) %collective-permute-start.3) | collective-permute-done | bytes 262176 | tf_op jit(solution)/shard_map/ppermute | solution.py:35
  19.5 0.1 add_convert_fusion.4
  19.6 0.0 copy-start.4
  19.6 2.8 %collective-permute-start.4 = (bf16[32,4096]{1,0:T(8,128)(2,1)S(1)}, bf16[32,4096]{1,0:T(8,128)(2,1)S(1)}, u32[]{:S(2)}, u32[]{:S(2)}) collective-permute-start(bf16[32,4096]{1,0:T(8,128)(2,1)S(1)} %add_convert_fusion.4), channel_id=1, source_target_pairs={{0,8},{1,9},{2,10},{3,11},{4,12},{5,13},{6,14},{7,15},{8,0},{9,1},... | collective-permute-start | bytes 786440 | tf_op jit(solution)/shard_map/ppermute | solution.py:35
  22.4 0.1 add_convert_fusion.3
  22.5 0.0 copy-start
  22.5 2.6 %collective-permute-done.6 = bf16[32,4096]{1,0:T(8,128)(2,1)S(1)} collective-permute-done((bf16[32,4096]{1,0:T(8,128)(2,1)S(1)}, bf16[32,4096]{1,0:T(8,128)(2,1)S(1)}, u32[]{:S(2)}, u32[]{:S(2)}) %collective-permute-start.6) | collective-permute-done | bytes 262176 | tf_op jit(solution)/shard_map/ppermute | solution.py:35
  25.1 0.1 add_convert_fusion.1
  25.2 1.3 %collective-permute-start.7 = (bf16[32,4096]{1,0:T(8,128)(2,1)S(1)}, bf16[32,4096]{1,0:T(8,128)(2,1)S(1)}, u32[]{:S(2)}, u32[]{:S(2)}) collective-permute-start(bf16[32,4096]{1,0:T(8,128)(2,1)S(1)} %add_convert_fusion.1), channel_id=1, source_target_pairs={{0,12},{1,5},{2,14},{3,7},{4,8},{5,1},{6,10},{7,3},{8,4},{9,13},{1... | collective-permute-start | bytes 786440 | tf_op jit(solution)/shard_map/ppermute | solution.py:35
  26.5 0.2 collective-permute-start.5
  26.7 0.2 collective-permute-done.4
  26.9 5.5 %collective-permute-done.7 = bf16[32,4096]{1,0:T(8,128)(2,1)S(1)} collective-permute-done((bf16[32,4096]{1,0:T(8,128)(2,1)S(1)}, bf16[32,4096]{1,0:T(8,128)(2,1)S(1)}, u32[]{:S(2)}, u32[]{:S(2)}) %collective-permute-start.7) | collective-permute-done | bytes 262176 | tf_op jit(solution)/shard_map/ppermute | solution.py:35
  32.4 0.2 fusion.18
  32.6 0.0 copy-start.3
  32.7 3.1 %collective-permute-start.8 = (bf16[32,4096]{1,0:T(8,128)(2,1)S(1)}, bf16[32,4096]{1,0:T(8,128)(2,1)S(1)}, u32[]{:S(2)}, u32[]{:S(2)}) collective-permute-start(bf16[32,4096]{1,0:T(8,128)(2,1)S(1)} %fusion.18), channel_id=1, source_target_pairs={{0,16},{16,32},{32,48},{48,0},{1,17},{17,33},{33,49},{49,1},{2,18}... | collective-permute-start | bytes 786440 | tf_op jit(solution)/shard_map/ppermute | solution.py:40
  35.7 13.0 %collective-permute-done.8 = bf16[32,4096]{1,0:T(8,128)(2,1)S(1)} collective-permute-done((bf16[32,4096]{1,0:T(8,128)(2,1)S(1)}, bf16[32,4096]{1,0:T(8,128)(2,1)S(1)}, u32[]{:S(2)}, u32[]{:S(2)}) %collective-permute-start.8) | collective-permute-done | bytes 262176 | tf_op jit(solution)/shard_map/ppermute | solution.py:40
  48.7 0.2 fusion.10
  48.9 0.1 fusion.12.refs_0_
  49.0 2.2 %collective-permute-start.10 = (bf16[32,4096]{1,0:T(8,128)(2,1)S(1)}, bf16[32,4096]{1,0:T(8,128)(2,1)}, u32[]{:S(2)}, u32[]{:S(2)}) collective-permute-start(bf16[32,4096]{1,0:T(8,128)(2,1)S(1)} %fusion.12.refs_0_), channel_id=1, source_target_pairs={{0,12},{1,5},{2,14},{3,7},{4,8},{5,1},{6,10},{7,3},{8,4},{9,13},{1... | collective-permute-start | bytes 786440 | tf_op jit(solution)/shard_map/ppermute | solution.py:35
  51.3 2.6 %collective-permute-start.11 = (bf16[32,4096]{1,0:T(8,128)(2,1)S(1)}, bf16[32,4096]{1,0:T(8,128)(2,1)}, u32[]{:S(2)}, u32[]{:S(2)}) collective-permute-start(bf16[32,4096]{1,0:T(8,128)(2,1)S(1)} %fusion.12.refs_0_), channel_id=1, source_target_pairs={{0,4},{1,13},{2,6},{3,15},{4,0},{5,9},{6,2},{7,11},{8,12},{9,5},{1... | collective-permute-start | bytes 786440 | tf_op jit(solution)/shard_map/ppermute | solution.py:35
  53.9 0.0 collective-permute-start.12
  53.9 0.2 collective-permute-start.9
  54.1 1.0 %collective-permute-done.10.refs_3_ = bf16[32,4096]{1,0:T(8,128)(2,1)} collective-permute-done((bf16[32,4096]{1,0:T(8,128)(2,1)S(1)}, bf16[32,4096]{1,0:T(8,128)(2,1)}, u32[]{:S(2)}, u32[]{:S(2)}) %collective-permute-start.10) | collective-permute-done | bytes 262176 | tf_op jit(solution)/shard_map/ppermute | solution.py:35
  55.2 10.3 %collective-permute-done.11.refs_2_ = bf16[32,4096]{1,0:T(8,128)(2,1)} collective-permute-done((bf16[32,4096]{1,0:T(8,128)(2,1)S(1)}, bf16[32,4096]{1,0:T(8,128)(2,1)}, u32[]{:S(2)}, u32[]{:S(2)}) %collective-permute-start.11) | collective-permute-done | bytes 262176 | tf_op jit(solution)/shard_map/ppermute | solution.py:35
  65.5 0.0 collective-permute-done.12.refs_4_
  65.5 0.0 collective-permute-done.9.refs_1_
  65.5 1.6 %collective-permute-start.17 = (bf16[32,4096]{1,0:T(8,128)(2,1)}, bf16[32,4096]{1,0:T(8,128)(2,1)}, u32[]{:S(2)}, u32[]{:S(2)}) collective-permute-start(bf16[32,4096]{1,0:T(8,128)(2,1)} %collective-permute-done.12.refs_4_), channel_id=1, source_target_pairs={{0,1},{1,0},{2,3},{3,2},{4,5},{5,4},{6,7},{7,6},{8,9},{9,8},{10,11... | collective-permute-start | bytes 786440 | tf_op jit(solution)/shard_map/ppermute | solution.py:35
  67.0 0.1 collective-permute-start.16
  67.1 0.4 collective-permute-start.15
  67.6 0.1 collective-permute-start.14
  67.7 0.4 collective-permute-start.13
  68.1 0.1 stack.87.ids
  68.2 0.4 collective-permute-done.17.refs_9_
  68.5 1.3 %collective-permute-start.20 = (bf16[32,4096]{1,0:T(8,128)(2,1)}, bf16[32,4096]{1,0:T(8,128)(2,1)S(1)}, u32[]{:S(2)}, u32[]{:S(2)}) collective-permute-start(bf16[32,4096]{1,0:T(8,128)(2,1)} %collective-permute-done.12.refs_4_), channel_id=1, source_target_pairs={{0,8},{1,9},{2,10},{3,11},{4,12},{5,13},{6,14},{7,15},{8,0},{9,1},... | collective-permute-start | bytes 786440 | tf_op jit(solution)/shard_map/ppermute | solution.py:35
  69.9 2.1 %collective-permute-start.18 = (bf16[32,4096]{1,0:T(8,128)(2,1)}, bf16[32,4096]{1,0:T(8,128)(2,1)S(1)}, u32[]{:S(2)}, u32[]{:S(2)}) collective-permute-start(bf16[32,4096]{1,0:T(8,128)(2,1)} %collective-permute-done.12.refs_4_), channel_id=1, source_target_pairs={{0,4},{1,13},{2,6},{3,15},{4,0},{5,9},{6,2},{7,11},{8,12},{9,5},{1... | collective-permute-start | bytes 786440 | tf_op jit(solution)/shard_map/ppermute | solution.py:35
  71.9 0.0 collective-permute-done.14.refs_6_
  71.9 0.0 collective-permute-done.13.refs_5_
  72.0 4.5 %shard_map.69 = (bf16[512,384]{1,0:T(8,128)(2,1)}, f32[8,128]{1,0:T(8,128)}) custom-call(s32[16]{0:T(128)S(1)} %stack.87.ids, bf16[4096,384]{1,0:T(8,128)(2,1)S(1)} %bitcast.35, bf16[32,4096]{1,0:T(8,128)(2,1)S(1)} %fusion.12.refs_0_, bf16[32,4096]{1,0:T(8,128)(2,1)} %collective-permute-done.9.refs_1_, bf16[32,4096]{1,0:T(8,128)(2,1)} %collective-permute-done.11.refs_2_, ...), custom_call_target="tpu_custom_call" | custom-call | flops 20132659200 | bytes 6012928 | tf_op jit(solution)/shard_map/pallas_call | solution.py:122
  76.4 1.4 %collective-permute-done.20.refs_3_ = bf16[32,4096]{1,0:T(8,128)(2,1)S(1)} collective-permute-done((bf16[32,4096]{1,0:T(8,128)(2,1)}, bf16[32,4096]{1,0:T(8,128)(2,1)S(1)}, u32[]{:S(2)}, u32[]{:S(2)}) %collective-permute-start.20) | collective-permute-done | bytes 262176 | tf_op jit(solution)/shard_map/ppermute | solution.py:35
  77.8 1.3 %collective-permute-start.23 = (bf16[32,4096]{1,0:T(8,128)(2,1)S(1)}, bf16[32,4096]{1,0:T(8,128)(2,1)S(1)}, u32[]{:S(2)}, u32[]{:S(2)}) collective-permute-start(bf16[32,4096]{1,0:T(8,128)(2,1)S(1)} %collective-permute-done.20.refs_3_), channel_id=1, source_target_pairs={{0,1},{1,0},{2,3},{3,2},{4,5},{5,4},{6,7},{7,6},{8,9},{9,8},{10,11... | collective-permute-start | bytes 786440 | tf_op jit(solution)/shard_map/ppermute | solution.py:35
  79.1 0.0 collective-permute-done.19.refs_2_
  79.1 0.0 collective-permute-start.22
  79.1 2.0 %collective-permute-done.18.refs_1_ = bf16[32,4096]{1,0:T(8,128)(2,1)S(1)} collective-permute-done((bf16[32,4096]{1,0:T(8,128)(2,1)}, bf16[32,4096]{1,0:T(8,128)(2,1)S(1)}, u32[]{:S(2)}, u32[]{:S(2)}) %collective-permute-start.18) | collective-permute-done | bytes 262176 | tf_op jit(solution)/shard_map/ppermute | solution.py:35
  81.1 1.0 %collective-permute-start.21 = (bf16[32,4096]{1,0:T(8,128)(2,1)S(1)}, bf16[32,4096]{1,0:T(8,128)(2,1)S(1)}, u32[]{:S(2)}, u32[]{:S(2)}) collective-permute-start(bf16[32,4096]{1,0:T(8,128)(2,1)S(1)} %collective-permute-done.18.refs_1_), channel_id=1, source_target_pairs={{0,1},{1,0},{2,3},{3,2},{4,5},{5,4},{6,7},{7,6},{8,9},{9,8},{10,11... | collective-permute-start | bytes 786440 | tf_op jit(solution)/shard_map/ppermute | solution.py:35
  82.1 1.2 %collective-permute-done.21.refs_4_ = bf16[32,4096]{1,0:T(8,128)(2,1)S(1)} collective-permute-done((bf16[32,4096]{1,0:T(8,128)(2,1)S(1)}, bf16[32,4096]{1,0:T(8,128)(2,1)S(1)}, u32[]{:S(2)}, u32[]{:S(2)}) %collective-permute-start.21) | collective-permute-done | bytes 262176 | tf_op jit(solution)/shard_map/ppermute | solution.py:35
  83.2 2.8 %shard_map.70 = (bf16[512,384]{1,0:T(8,128)(2,1)}, f32[8,128]{1,0:T(8,128)}) custom-call(s32[16]{0:T(128)S(1)} %stack.87.ids, bf16[4096,384]{1,0:T(8,128)(2,1)S(1)} %bitcast.36, bf16[512,384]{1,0:T(8,128)(2,1)} %get-tuple-element.26.refs_0_, bf16[32,4096]{1,0:T(8,128)(2,1)S(1)} %collective-permute-done.18.refs_1_, ...), custom_call_target="tpu_custom_call", output_to_operand_aliasing={{0}: (2, {})} | custom-call | flops 603979776 | bytes 4866048 | tf_op jit(solution)/shard_map/pallas_call | solution.py:122
  (16 shorter events, 0.0 us)
Async XLA Ops:
  0.8 1.2 %copy-start.1 = (bf16[1,512,896]{2,1,0:T(8,128)(2,1)S(1)}, bf16[1,512,896]{2,1,0:T(8,128)(2,1)}, u32[]{:S(2)}) copy-start(bf16[1,512,896]{2,1,0:T(8,128)(2,1)} %param.5) | copy-start | bytes 2752516
  2.0 7.5 %slice-start = ((s8[7340032]{0:T(1024)(128)(4,1)}), s8[4194304]{0:T(1024)(128)(4,1)S(1)}, s32[]{:S(2)}) async-start(s8[7340032]{0:T(1024)(128)(4,1)} %bitcast.41), calls=%async_computation | async-start | bytes 8388608
  2.6 6.8 %slice-start.1 = ((s8[7340032]{0:T(1024)(128)(4,1)}), s8[3145728]{0:T(1024)(128)(4,1)S(1)}, s32[]{:S(2)}) async-start(s8[7340032]{0:T(1024)(128)(4,1)} %bitcast.41), calls=%async_computation.1 | async-start | bytes 6291456
  8.5 3.2 %collective-permute-start.1 = (bf16[128,4096]{1,0:T(8,128)(2,1)S(1)}, bf16[128,4096]{1,0:T(8,128)(2,1)S(1)}, u32[]{:S(2)}, u32[]{:S(2)}) collective-permute-start(bf16[128,4096]{1,0:T(8,128)(2,1)S(1)} %get-tuple-element.35), channel_id=1, source_target_pairs={{0,1},{1,0},{2,3},{3,2},{4,5},{5,4},{6,7},{7,6},{8,9},{9,8},{10,11... | collective-permute-start | bytes 3145736 | tf_op jit(solution)/shard_map/ppermute | solution.py:35
  9.3 6.9 %collective-permute-start = (bf16[128,4096]{1,0:T(8,128)(2,1)S(1)}, bf16[128,4096]{1,0:T(8,128)(2,1)S(1)}, u32[]{:S(2)}, u32[]{:S(2)}) collective-permute-start(bf16[128,4096]{1,0:T(8,128)(2,1)S(1)} %get-tuple-element.34), channel_id=1, source_target_pairs={{0,1},{1,0},{2,3},{3,2},{4,5},{5,4},{6,7},{7,6},{8,9},{9,8},{10,11... | collective-permute-start | bytes 3145736 | tf_op jit(solution)/shard_map/ppermute | solution.py:35
  11.9 20.5 %copy-start.2 = (bf16[1,32,4096]{2,1,0:T(8,128)(2,1)S(1)}, bf16[1,32,4096]{2,1,0:T(8,128)(2,1)}, u32[]{:S(2)}) copy-start(bf16[1,32,4096]{2,1,0:T(8,128)(2,1)} %param.6) | copy-start | bytes 786436
  11.9 7.6 %collective-permute-start.3 = (bf16[32,4096]{1,0:T(8,128)(2,1)S(1)}, bf16[32,4096]{1,0:T(8,128)(2,1)S(1)}, u32[]{:S(2)}, u32[]{:S(2)}) collective-permute-start(bf16[32,4096]{1,0:T(8,128)(2,1)S(1)} %get-tuple-element.32), channel_id=1, source_target_pairs={{0,2},{1,3},{2,0},{3,1},{4,6},{5,7},{6,4},{7,5},{8,10},{9,11},{10,... | collective-permute-start | bytes 786440 | tf_op jit(solution)/shard_map/ppermute | solution.py:35
  12.1 10.3 %collective-permute-start.2 = (bf16[64,4096]{1,0:T(8,128)(2,1)S(1)}, bf16[64,4096]{1,0:T(8,128)(2,1)S(1)}, u32[]{:S(2)}, u32[]{:S(2)}) collective-permute-start(bf16[64,4096]{1,0:T(8,128)(2,1)S(1)} %add_convert_fusion), channel_id=1, source_target_pairs={{0,4},{1,13},{2,6},{3,15},{4,0},{5,9},{6,2},{7,11},{8,12},{9,5},{1... | collective-permute-start | bytes 1572872 | tf_op jit(solution)/shard_map/ppermute | solution.py:35
  14.7 10.4 %collective-permute-start.6 = (bf16[32,4096]{1,0:T(8,128)(2,1)S(1)}, bf16[32,4096]{1,0:T(8,128)(2,1)S(1)}, u32[]{:S(2)}, u32[]{:S(2)}) collective-permute-start(bf16[32,4096]{1,0:T(8,128)(2,1)S(1)} %get-tuple-element.33), channel_id=1, source_target_pairs={{0,2},{1,3},{2,0},{3,1},{4,6},{5,7},{6,4},{7,5},{8,10},{9,11},{10,... | collective-permute-start | bytes 786440 | tf_op jit(solution)/shard_map/ppermute | solution.py:35
  19.6 29.3 %copy-start.4 = (f32[1,4096]{1,0:T(1,128)S(1)}, f32[1,4096]{1,0:T(1,128)}, u32[]{:S(2)}) copy-start(f32[1,4096]{1,0:T(1,128)} %param.7) | copy-start | bytes 49156
  19.6 7.3 %collective-permute-start.4 = (bf16[32,4096]{1,0:T(8,128)(2,1)S(1)}, bf16[32,4096]{1,0:T(8,128)(2,1)S(1)}, u32[]{:S(2)}, u32[]{:S(2)}) collective-permute-start(bf16[32,4096]{1,0:T(8,128)(2,1)S(1)} %add_convert_fusion.4), channel_id=1, source_target_pairs={{0,8},{1,9},{2,10},{3,11},{4,12},{5,13},{6,14},{7,15},{8,0},{9,1},... | collective-permute-start | bytes 786440 | tf_op jit(solution)/shard_map/ppermute | solution.py:35
  22.5 49.4 %copy-start = (bf16[1,4096,384]{2,1,0:T(8,128)(2,1)S(1)}, bf16[1,4096,384]{2,1,0:T(8,128)(2,1)}, u32[]{:S(2)}) copy-start(bf16[1,4096,384]{2,1,0:T(8,128)(2,1)} %param.9) | copy-start | bytes 9437188
  25.2 7.2 %collective-permute-start.7 = (bf16[32,4096]{1,0:T(8,128)(2,1)S(1)}, bf16[32,4096]{1,0:T(8,128)(2,1)S(1)}, u32[]{:S(2)}, u32[]{:S(2)}) collective-permute-start(bf16[32,4096]{1,0:T(8,128)(2,1)S(1)} %add_convert_fusion.1), channel_id=1, source_target_pairs={{0,12},{1,5},{2,14},{3,7},{4,8},{5,1},{6,10},{7,3},{8,4},{9,13},{1... | collective-permute-start | bytes 786440 | tf_op jit(solution)/shard_map/ppermute | solution.py:35
  26.5 5.9 %collective-permute-start.5 = (bf16[32,4096]{1,0:T(8,128)(2,1)S(1)}, bf16[32,4096]{1,0:T(8,128)(2,1)S(1)}, u32[]{:S(2)}, u32[]{:S(2)}) collective-permute-start(bf16[32,4096]{1,0:T(8,128)(2,1)S(1)} %add_convert_fusion.3), channel_id=1, source_target_pairs={{0,2},{1,3},{2,0},{3,1},{4,6},{5,7},{6,4},{7,5},{8,10},{9,11},{10,... | collective-permute-start | bytes 786440 | tf_op jit(solution)/shard_map/ppermute | solution.py:35
  32.6 35.0 %copy-start.3 = (bf16[32,4096]{1,0:T(8,128)(2,1)}, bf16[32,4096]{1,0:T(8,128)(2,1)S(1)}, u32[]{:S(2)}) copy-start(bf16[32,4096]{1,0:T(8,128)(2,1)S(1)} %fusion.18) | copy-start | bytes 786436
  32.7 16.1 %collective-permute-start.8 = (bf16[32,4096]{1,0:T(8,128)(2,1)S(1)}, bf16[32,4096]{1,0:T(8,128)(2,1)S(1)}, u32[]{:S(2)}, u32[]{:S(2)}) collective-permute-start(bf16[32,4096]{1,0:T(8,128)(2,1)S(1)} %fusion.18), channel_id=1, source_target_pairs={{0,16},{16,32},{32,48},{48,0},{1,17},{17,33},{33,49},{49,1},{2,18}... | collective-permute-start | bytes 786440 | tf_op jit(solution)/shard_map/ppermute | solution.py:40
  49.0 6.1 %collective-permute-start.10 = (bf16[32,4096]{1,0:T(8,128)(2,1)S(1)}, bf16[32,4096]{1,0:T(8,128)(2,1)}, u32[]{:S(2)}, u32[]{:S(2)}) collective-permute-start(bf16[32,4096]{1,0:T(8,128)(2,1)S(1)} %fusion.12.refs_0_), channel_id=1, source_target_pairs={{0,12},{1,5},{2,14},{3,7},{4,8},{5,1},{6,10},{7,3},{8,4},{9,13},{1... | collective-permute-start | bytes 786440 | tf_op jit(solution)/shard_map/ppermute | solution.py:35
  51.3 14.2 %collective-permute-start.11 = (bf16[32,4096]{1,0:T(8,128)(2,1)S(1)}, bf16[32,4096]{1,0:T(8,128)(2,1)}, u32[]{:S(2)}, u32[]{:S(2)}) collective-permute-start(bf16[32,4096]{1,0:T(8,128)(2,1)S(1)} %fusion.12.refs_0_), channel_id=1, source_target_pairs={{0,4},{1,13},{2,6},{3,15},{4,0},{5,9},{6,2},{7,11},{8,12},{9,5},{1... | collective-permute-start | bytes 786440 | tf_op jit(solution)/shard_map/ppermute | solution.py:35
  53.9 11.5 %collective-permute-start.12 = (bf16[32,4096]{1,0:T(8,128)(2,1)S(1)}, bf16[32,4096]{1,0:T(8,128)(2,1)}, u32[]{:S(2)}, u32[]{:S(2)}) collective-permute-start(bf16[32,4096]{1,0:T(8,128)(2,1)S(1)} %fusion.12.refs_0_), channel_id=1, source_target_pairs={{0,2},{1,3},{2,0},{3,1},{4,6},{5,7},{6,4},{7,5},{8,10},{9,11},{10,... | collective-permute-start | bytes 786440 | tf_op jit(solution)/shard_map/ppermute | solution.py:35
  53.9 11.5 %collective-permute-start.9 = (bf16[32,4096]{1,0:T(8,128)(2,1)S(1)}, bf16[32,4096]{1,0:T(8,128)(2,1)}, u32[]{:S(2)}, u32[]{:S(2)}) collective-permute-start(bf16[32,4096]{1,0:T(8,128)(2,1)S(1)} %fusion.12.refs_0_), channel_id=1, source_target_pairs={{0,8},{1,9},{2,10},{3,11},{4,12},{5,13},{6,14},{7,15},{8,0},{9,1},... | collective-permute-start | bytes 786440 | tf_op jit(solution)/shard_map/ppermute | solution.py:35
  65.5 3.1 %collective-permute-start.17 = (bf16[32,4096]{1,0:T(8,128)(2,1)}, bf16[32,4096]{1,0:T(8,128)(2,1)}, u32[]{:S(2)}, u32[]{:S(2)}) collective-permute-start(bf16[32,4096]{1,0:T(8,128)(2,1)} %collective-permute-done.12.refs_4_), channel_id=1, source_target_pairs={{0,1},{1,0},{2,3},{3,2},{4,5},{5,4},{6,7},{7,6},{8,9},{9,8},{10,11... | collective-permute-start | bytes 786440 | tf_op jit(solution)/shard_map/ppermute | solution.py:35
  67.0 2.8 %collective-permute-start.16 = (bf16[32,4096]{1,0:T(8,128)(2,1)}, bf16[32,4096]{1,0:T(8,128)(2,1)}, u32[]{:S(2)}, u32[]{:S(2)}) collective-permute-start(bf16[32,4096]{1,0:T(8,128)(2,1)} %collective-permute-done.10.refs_3_), channel_id=1, source_target_pairs={{0,1},{1,0},{2,3},{3,2},{4,5},{5,4},{6,7},{7,6},{8,9},{9,8},{10,11... | collective-permute-start | bytes 786440 | tf_op jit(solution)/shard_map/ppermute | solution.py:35
  67.1 2.7 %collective-permute-start.15 = (bf16[32,4096]{1,0:T(8,128)(2,1)}, bf16[32,4096]{1,0:T(8,128)(2,1)}, u32[]{:S(2)}, u32[]{:S(2)}) collective-permute-start(bf16[32,4096]{1,0:T(8,128)(2,1)} %collective-permute-done.11.refs_2_), channel_id=1, source_target_pairs={{0,1},{1,0},{2,3},{3,2},{4,5},{5,4},{6,7},{7,6},{8,9},{9,8},{10,11... | collective-permute-start | bytes 786440 | tf_op jit(solution)/shard_map/ppermute | solution.py:35
  67.6 4.4 %collective-permute-start.14 = (bf16[32,4096]{1,0:T(8,128)(2,1)}, bf16[32,4096]{1,0:T(8,128)(2,1)}, u32[]{:S(2)}, u32[]{:S(2)}) collective-permute-start(bf16[32,4096]{1,0:T(8,128)(2,1)} %collective-permute-done.9.refs_1_), channel_id=1, source_target_pairs={{0,1},{1,0},{2,3},{3,2},{4,5},{5,4},{6,7},{7,6},{8,9},{9,8},{10,11... | collective-permute-start | bytes 786440 | tf_op jit(solution)/shard_map/ppermute | solution.py:35
  67.7 4.3 %collective-permute-start.13 = (bf16[32,4096]{1,0:T(8,128)(2,1)S(1)}, bf16[32,4096]{1,0:T(8,128)(2,1)}, u32[]{:S(2)}, u32[]{:S(2)}) collective-permute-start(bf16[32,4096]{1,0:T(8,128)(2,1)S(1)} %fusion.12.refs_0_), channel_id=1, source_target_pairs={{0,1},{1,0},{2,3},{3,2},{4,5},{5,4},{6,7},{7,6},{8,9},{9,8},{10,11... | collective-permute-start | bytes 786440 | tf_op jit(solution)/shard_map/ppermute | solution.py:35
  68.5 9.3 %collective-permute-start.20 = (bf16[32,4096]{1,0:T(8,128)(2,1)}, bf16[32,4096]{1,0:T(8,128)(2,1)S(1)}, u32[]{:S(2)}, u32[]{:S(2)}) collective-permute-start(bf16[32,4096]{1,0:T(8,128)(2,1)} %collective-permute-done.12.refs_4_), channel_id=1, source_target_pairs={{0,8},{1,9},{2,10},{3,11},{4,12},{5,13},{6,14},{7,15},{8,0},{9,1},... | collective-permute-start | bytes 786440 | tf_op jit(solution)/shard_map/ppermute | solution.py:35
  69.9 9.2 %collective-permute-start.19 = (bf16[32,4096]{1,0:T(8,128)(2,1)}, bf16[32,4096]{1,0:T(8,128)(2,1)S(1)}, u32[]{:S(2)}, u32[]{:S(2)}) collective-permute-start(bf16[32,4096]{1,0:T(8,128)(2,1)} %collective-permute-done.10.refs_3_), channel_id=1, source_target_pairs={{0,2},{1,3},{2,0},{3,1},{4,6},{5,7},{6,4},{7,5},{8,10},{9,11},{10,... | collective-permute-start | bytes 786440 | tf_op jit(solution)/shard_map/ppermute | solution.py:35
  69.9 11.2 %collective-permute-start.18 = (bf16[32,4096]{1,0:T(8,128)(2,1)}, bf16[32,4096]{1,0:T(8,128)(2,1)S(1)}, u32[]{:S(2)}, u32[]{:S(2)}) collective-permute-start(bf16[32,4096]{1,0:T(8,128)(2,1)} %collective-permute-done.12.refs_4_), channel_id=1, source_target_pairs={{0,4},{1,13},{2,6},{3,15},{4,0},{5,9},{6,2},{7,11},{8,12},{9,5},{1... | collective-permute-start | bytes 786440 | tf_op jit(solution)/shard_map/ppermute | solution.py:35
  77.8 4.3 %collective-permute-start.23 = (bf16[32,4096]{1,0:T(8,128)(2,1)S(1)}, bf16[32,4096]{1,0:T(8,128)(2,1)S(1)}, u32[]{:S(2)}, u32[]{:S(2)}) collective-permute-start(bf16[32,4096]{1,0:T(8,128)(2,1)S(1)} %collective-permute-done.20.refs_3_), channel_id=1, source_target_pairs={{0,1},{1,0},{2,3},{3,2},{4,5},{5,4},{6,7},{7,6},{8,9},{9,8},{10,11... | collective-permute-start | bytes 786440 | tf_op jit(solution)/shard_map/ppermute | solution.py:35
  79.1 3.0 %collective-permute-start.22 = (bf16[32,4096]{1,0:T(8,128)(2,1)S(1)}, bf16[32,4096]{1,0:T(8,128)(2,1)S(1)}, u32[]{:S(2)}, u32[]{:S(2)}) collective-permute-start(bf16[32,4096]{1,0:T(8,128)(2,1)S(1)} %collective-permute-done.19.refs_2_), channel_id=1, source_target_pairs={{0,1},{1,0},{2,3},{3,2},{4,5},{5,4},{6,7},{7,6},{8,9},{9,8},{10,11... | collective-permute-start | bytes 786440 | tf_op jit(solution)/shard_map/ppermute | solution.py:35
  81.1 2.1 %collective-permute-start.21 = (bf16[32,4096]{1,0:T(8,128)(2,1)S(1)}, bf16[32,4096]{1,0:T(8,128)(2,1)S(1)}, u32[]{:S(2)}, u32[]{:S(2)}) collective-permute-start(bf16[32,4096]{1,0:T(8,128)(2,1)S(1)} %collective-permute-done.18.refs_1_), channel_id=1, source_target_pairs={{0,1},{1,0},{2,3},{3,2},{4,5},{5,4},{6,7},{7,6},{8,9},{9,8},{10,11... | collective-permute-start | bytes 786440 | tf_op jit(solution)/shard_map/ppermute | solution.py:35

commit v3 on v2

--- a/solution.py
+++ b/solution.py
@@ -92,9 +92,10 @@
     return total.astype(jnp.bfloat16)
 
 
-def project_kernel(places, ids, w_ref, *refs):
-    out_ref, ready_ref, rows_ref, sem = refs[-4:]
-    parts = refs[:-4] if len(places) == len(refs) - 4 else refs[1:-4]
+def project_kernel(places, first, ids, w_ref, *refs):
+    rows_ref, sem = refs[-2:]
+    parts = refs[:-4] if first else refs[1:-3]
+    out_ref = refs[-4] if first else refs[-3]
     rows = rows_ref.shape[0] // len(places)
     rows_ref[...] = product(parts, w_ref)
     copies = []
@@ -107,7 +108,8 @@
         )
     for c in copies:
         c.start()
-    ready_ref[...] = jnp.zeros_like(ready_ref)
+    if first:
+        refs[-3][...] = jnp.zeros_like(refs[-3])
     for c in copies:
         c.wait()
 
@@ -120,13 +122,13 @@
     vmem = pl.BlockSpec(memory_space=pltpu.VMEM)
     anywhere = pl.BlockSpec(memory_space=pl.ANY)
     return pl.pallas_call(
-        functools.partial(project_kernel, places),
+        functools.partial(project_kernel, places, before is None),
         out_shape=[
             jax.ShapeDtypeStruct((16 * rows, width), jnp.bfloat16),
             jax.ShapeDtypeStruct((8, 128), jnp.float32),
-        ],
+        ][: 2 - len(extra)],
         in_specs=[pl.BlockSpec(memory_space=pltpu.SMEM), vmem] + [anywhere] * len(extra) + [vmem] * n,
-        out_specs=[anywhere, vmem],
+        out_specs=[anywhere, vmem][: 2 - len(extra)],
         scratch_shapes=[
             pltpu.VMEM((n * rows, width), jnp.bfloat16),
             pltpu.SemaphoreType.DMA((n,)),
@@ -184,21 +186,20 @@
     out = lax.optimization_barrier(out)
 
     normed = lax.optimization_barrier(normalize(next_section(out), gain))
-    ab = trade(normed, "ab")
+    b = trade(normed, "b")
     z = trade(normed, "z")
-    b = trade(normed, "b")
     a = trade(normed, "a")
+    abz = trade(z, "ab")
     az = trade(z, "a")
-    abz = trade(z, "ab")
+    ab = trade(b, "a")
     bz = trade(b, "z")
-    near = [after(t, ab, b, a) for t in (normed, ab, a, b, z)]
-    near_swap = [trade(t, "core") for t in near]
-    near_places = (0, 1, 2, 3, 4, 8, 9, 10, 11, 12)
-    rows_near, ready = project(near + near_swap, near_places, out_ids, qkv, weight=20)
-    late = [after(t, ready) for t in (az, bz, abz)]
+    near = [after(t, a, b, z) for t in (normed, a, b, z)]
+    rows_near, ready = project(near, (0, 2, 3, 4), out_ids, qkv, weight=20)
+    near_swap = [trade(after(t, ready), "core") for t in near]
+    late = [after(t, ready) for t in (ab, bz, az, abz)]
     late_swap = [trade(t, "core") for t in late]
-    late_places = (5, 7, 6, 13, 15, 14)
-    proj, _ = project(late + late_swap, late_places, out_ids, qkv, before=rows_near)
+    places = (8, 10, 11, 12, 1, 7, 5, 6, 9, 15, 13, 14)
+    (proj,) = project(near_swap + late + late_swap, places, out_ids, qkv, before=rows_near)
     return (out[None], proj[None])
 
 

time: 86.4 us -> 83.3 us (0.964)
  waiting for transfers between devices: 40.9 us -> 36.1 us
  starting transfers between devices: 25.7 us -> 27.9 us
  Pallas kernels: 7.9 us -> 6.83 us
    ppermute x23, waiting for transfers between devices: 27.9 us -> 23.1 us  [trade(): return lax.ppermute(value, AXES, pairs)]
    ppermute x23, starting transfers between devices: 22.6 us -> 24.9 us  [trade(): return lax.ppermute(value, AXES, pairs)]
    pallas_call x2, Pallas kernels: 7.28 us -> 6.21 us  [project(): pl.pallas_call(functools.partial(project_kernel, places, before is None),...]
  transfers between devices with their start and end apart: 24 -> 24, of which waited for: 11 -> 15; matrix products, arithmetic and copies ran while one was open for 3% -> 4% of each run, Pallas kernels for 5% -> 4%
where the time goes in v3:
time: 83.3 us; the launch traced here: 82.7 us
  waiting for transfers between devices  36.1 us (43%)
  starting transfers between devices  27.9 us (33%)
  matrix products  8.06 us (10%)
  Pallas kernels  6.83 us (8%)
  local copies, waits for them, and re-layouts  1.61 us (2%)
  other arithmetic  1.09 us (1%)
  between operations  1.03 us (1%)
    ppermute x23, starting transfers between devices, trade(): return lax.ppermute(value, AXES, pairs)  24.9 us
    ppermute x23, waiting for transfers between devices, trade(): return lax.ppermute(value, AXES, pairs)  23.1 us
    ppermute x1, waiting for transfers between devices, next_section(): lax.ppermute(value, 'pipe', [(s, (s + 1) % count) for s in range(count)])  13 us
    dot_general x2, matrix products, dot_bf16(): jnp.dot(a, b, preferred_element_type=jnp.float32).astype(jnp.bfloat16)  8.06 us
    pallas_call x2, Pallas kernels, project(): pl.pallas_call(functools.partial(project_kernel, places, before is None),...  6.21 us
    ppermute x1, starting transfers between devices, next_section(): lax.ppermute(value, 'pipe', [(s, (s + 1) % count) for s in range(count)])  3.07 us
  transfers between devices with their start and end apart: 24, of which 15 were waited for; matrix products, arithmetic and copies ran while one was open for 4% of the time, Pallas kernels for 4%

profile of v3, /device:TPU:41, one launch (start us, length us, event | category | flops | bytes accessed | tf_op | source)
XLA Modules:
  0.0 82.7 jit_solution(14413955199687203748)
XLA Ops:
  0.7 0.1 stack.86.ids
  0.8 0.0 copy-start.1
  0.8 1.2 %copy-done.1 = bf16[1,512,896]{2,1,0:T(8,128)(2,1)S(1)} copy-done((bf16[1,512,896]{2,1,0:T(8,128)(2,1)S(1)}, bf16[1,512,896]{2,1,0:T(8,128)(2,1)}, u32[]{:S(2)}) %copy-start.1) | copy-done | bytes 917528
  2.0 0.6 shard_map.68
  2.6 0.0 slice-start.1
  2.6 5.7 %fusion.7 = bf16[256,4096]{1,0:T(8,128)(2,1)S(1)} fusion(bf16[256,896]{1,0:T(8,128)(2,1)S(1)} %get-tuple-element.21, bf16[1,896,4096]{2,1,0:T(8,128)(2,1)} %param.8), kind=kOutput, calls=%fused_computation.5 | convolution fusion | flops 1880096768 | bytes 9895936 | tf_op jit(solution)/shard_map/dot_general | solution.py:147
  8.3 0.2 fusion.19
  8.5 0.8 collective-permute-start.1
  9.3 0.1 collective-permute-start
  9.4 2.3 %fusion.4 = bf16[256,4096]{1,0:T(8,128)(2,1)S(1)} fusion(bf16[256,896]{1,0:T(8,128)(2,1)S(1)} %get-tuple-element.20, bf16[1,896,4096]{2,1,0:T(8,128)(2,1)S(1)} %bitcast.42), kind=kOutput, calls=%fused_computation.4 | convolution fusion | flops 1880096768 | bytes 9895936 | tf_op jit(solution)/shard_map/dot_general | solution.py:147
  11.8 0.0 collective-permute-done.1
  11.8 0.1 add_convert_fusion.5
  11.9 0.0 copy-start.2
  11.9 0.1 collective-permute-start.3
  12.0 0.1 add_convert_fusion
  12.1 2.6 %collective-permute-start.2 = (bf16[64,4096]{1,0:T(8,128)(2,1)S(1)}, bf16[64,4096]{1,0:T(8,128)(2,1)S(1)}, u32[]{:S(2)}, u32[]{:S(2)}) collective-permute-start(bf16[64,4096]{1,0:T(8,128)(2,1)S(1)} %add_convert_fusion), channel_id=1, source_target_pairs={{0,4},{1,13},{2,6},{3,15},{4,0},{5,9},{6,2},{7,11},{8,12},{9,5},{1... | collective-permute-start | bytes 1572872 | tf_op jit(solution)/shard_map/ppermute | solution.py:35
  14.7 1.4 %collective-permute-start.6 = (bf16[32,4096]{1,0:T(8,128)(2,1)S(1)}, bf16[32,4096]{1,0:T(8,128)(2,1)S(1)}, u32[]{:S(2)}, u32[]{:S(2)}) collective-permute-start(bf16[32,4096]{1,0:T(8,128)(2,1)S(1)} %get-tuple-element.39), channel_id=1, source_target_pairs={{0,2},{1,3},{2,0},{3,1},{4,6},{5,7},{6,4},{7,5},{8,10},{9,11},{10,... | collective-permute-start | bytes 786440 | tf_op jit(solution)/shard_map/ppermute | solution.py:35
  16.2 0.0 collective-permute-done
  16.2 3.3 %collective-permute-done.3 = bf16[32,4096]{1,0:T(8,128)(2,1)S(1)} collective-permute-done((bf16[32,4096]{1,0:T(8,128)(2,1)S(1)}, bf16[32,4096]{1,0:T(8,128)(2,1)S(1)}, u32[]{:S(2)}, u32[]{:S(2)}) %collective-permute-start.3) | collective-permute-done | bytes 262176 | tf_op jit(solution)/shard_map/ppermute | solution.py:35
  19.5 0.1 add_convert_fusion.4
  19.6 0.0 copy-start.4
  19.6 2.8 %collective-permute-start.4 = (bf16[32,4096]{1,0:T(8,128)(2,1)S(1)}, bf16[32,4096]{1,0:T(8,128)(2,1)S(1)}, u32[]{:S(2)}, u32[]{:S(2)}) collective-permute-start(bf16[32,4096]{1,0:T(8,128)(2,1)S(1)} %add_convert_fusion.4), channel_id=1, source_target_pairs={{0,8},{1,9},{2,10},{3,11},{4,12},{5,13},{6,14},{7,15},{8,0},{9,1},... | collective-permute-start | bytes 786440 | tf_op jit(solution)/shard_map/ppermute | solution.py:35
  22.4 0.1 add_convert_fusion.3
  22.5 0.0 copy-start
  22.5 2.6 %collective-permute-done.6 = bf16[32,4096]{1,0:T(8,128)(2,1)S(1)} collective-permute-done((bf16[32,4096]{1,0:T(8,128)(2,1)S(1)}, bf16[32,4096]{1,0:T(8,128)(2,1)S(1)}, u32[]{:S(2)}, u32[]{:S(2)}) %collective-permute-start.6) | collective-permute-done | bytes 262176 | tf_op jit(solution)/shard_map/ppermute | solution.py:35
  25.1 0.1 add_convert_fusion.1
  25.2 1.3 %collective-permute-start.7 = (bf16[32,4096]{1,0:T(8,128)(2,1)S(1)}, bf16[32,4096]{1,0:T(8,128)(2,1)S(1)}, u32[]{:S(2)}, u32[]{:S(2)}) collective-permute-start(bf16[32,4096]{1,0:T(8,128)(2,1)S(1)} %add_convert_fusion.1), channel_id=1, source_target_pairs={{0,12},{1,5},{2,14},{3,7},{4,8},{5,1},{6,10},{7,3},{8,4},{9,13},{1... | collective-permute-start | bytes 786440 | tf_op jit(solution)/shard_map/ppermute | solution.py:35
  26.5 0.2 collective-permute-start.5
  26.7 0.2 collective-permute-done.4
  26.9 5.5 %collective-permute-done.7 = bf16[32,4096]{1,0:T(8,128)(2,1)S(1)} collective-permute-done((bf16[32,4096]{1,0:T(8,128)(2,1)S(1)}, bf16[32,4096]{1,0:T(8,128)(2,1)S(1)}, u32[]{:S(2)}, u32[]{:S(2)}) %collective-permute-start.7) | collective-permute-done | bytes 262176 | tf_op jit(solution)/shard_map/ppermute | solution.py:35
  32.4 0.0 collective-permute-done.5
  32.4 0.2 fusion.18
  32.6 0.0 copy-start.3
  32.7 3.1 %collective-permute-start.8 = (bf16[32,4096]{1,0:T(8,128)(2,1)S(1)}, bf16[32,4096]{1,0:T(8,128)(2,1)S(1)}, u32[]{:S(2)}, u32[]{:S(2)}) collective-permute-start(bf16[32,4096]{1,0:T(8,128)(2,1)S(1)} %fusion.18), channel_id=1, source_target_pairs={{0,16},{16,32},{32,48},{48,0},{1,17},{17,33},{33,49},{49,1},{2,18}... | collective-permute-start | bytes 786440 | tf_op jit(solution)/shard_map/ppermute | solution.py:40
  35.7 13.0 %collective-permute-done.8 = bf16[32,4096]{1,0:T(8,128)(2,1)S(1)} collective-permute-done((bf16[32,4096]{1,0:T(8,128)(2,1)S(1)}, bf16[32,4096]{1,0:T(8,128)(2,1)S(1)}, u32[]{:S(2)}, u32[]{:S(2)}) %collective-permute-start.8) | collective-permute-done | bytes 262176 | tf_op jit(solution)/shard_map/ppermute | solution.py:40
  48.7 0.2 fusion.10
  48.9 0.1 fusion.12.refs_0_
  49.0 2.2 %collective-permute-start.10 = (bf16[32,4096]{1,0:T(8,128)(2,1)S(1)}, bf16[32,4096]{1,0:T(8,128)(2,1)}, u32[]{:S(2)}, u32[]{:S(2)}) collective-permute-start(bf16[32,4096]{1,0:T(8,128)(2,1)S(1)} %fusion.12.refs_0_), channel_id=1, source_target_pairs={{0,12},{1,5},{2,14},{3,7},{4,8},{5,1},{6,10},{7,3},{8,4},{9,13},{1... | collective-permute-start | bytes 786440 | tf_op jit(solution)/shard_map/ppermute | solution.py:35
  51.3 2.6 %collective-permute-start.9 = (bf16[32,4096]{1,0:T(8,128)(2,1)S(1)}, bf16[32,4096]{1,0:T(8,128)(2,1)}, u32[]{:S(2)}, u32[]{:S(2)}) collective-permute-start(bf16[32,4096]{1,0:T(8,128)(2,1)S(1)} %fusion.12.refs_0_), channel_id=1, source_target_pairs={{0,4},{1,13},{2,6},{3,15},{4,0},{5,9},{6,2},{7,11},{8,12},{9,5},{1... | collective-permute-start | bytes 786440 | tf_op jit(solution)/shard_map/ppermute | solution.py:35
  53.9 0.1 stack.87.ids
  54.0 1.1 %collective-permute-done.10.refs_2_ = bf16[32,4096]{1,0:T(8,128)(2,1)} collective-permute-done((bf16[32,4096]{1,0:T(8,128)(2,1)S(1)}, bf16[32,4096]{1,0:T(8,128)(2,1)}, u32[]{:S(2)}, u32[]{:S(2)}) %collective-permute-start.10) | collective-permute-done | bytes 262176 | tf_op jit(solution)/shard_map/ppermute | solution.py:35
  55.2 1.8 %collective-permute-done.11.refs_3_ = bf16[32,4096]{1,0:T(8,128)(2,1)} collective-permute-done((bf16[32,4096]{1,0:T(8,128)(2,1)S(1)}, bf16[32,4096]{1,0:T(8,128)(2,1)}, u32[]{:S(2)}, u32[]{:S(2)}) %collective-permute-start.11) | collective-permute-done | bytes 262176 | tf_op jit(solution)/shard_map/ppermute | solution.py:35
  56.9 3.7 %collective-permute-done.9.refs_1_ = bf16[32,4096]{1,0:T(8,128)(2,1)} collective-permute-done((bf16[32,4096]{1,0:T(8,128)(2,1)S(1)}, bf16[32,4096]{1,0:T(8,128)(2,1)}, u32[]{:S(2)}, u32[]{:S(2)}) %collective-permute-start.9) | collective-permute-done | bytes 262176 | tf_op jit(solution)/shard_map/ppermute | solution.py:35
  60.6 0.4 collective-permute-start.19
  61.0 2.4 %collective-permute-start.18 = (bf16[32,4096]{1,0:T(8,128)(2,1)}, bf16[32,4096]{1,0:T(8,128)(2,1)S(1)}, u32[]{:S(2)}, u32[]{:S(2)}) collective-permute-start(bf16[32,4096]{1,0:T(8,128)(2,1)} %collective-permute-done.11.refs_3_), channel_id=1, source_target_pairs={{0,4},{1,13},{2,6},{3,15},{4,0},{5,9},{6,2},{7,11},{8,12},{9,5},{1... | collective-permute-start | bytes 786440 | tf_op jit(solution)/shard_map/ppermute | solution.py:35
  63.4 3.1 %shard_map.69 = (bf16[512,384]{1,0:T(8,128)(2,1)}, f32[8,128]{1,0:T(8,128)}) custom-call(s32[16]{0:T(128)S(1)} %stack.87.ids, bf16[4096,384]{1,0:T(8,128)(2,1)S(1)} %bitcast.35, bf16[32,4096]{1,0:T(8,128)(2,1)S(1)} %fusion.12.refs_0_, bf16[32,4096]{1,0:T(8,128)(2,1)} %collective-permute-done.9.refs_1_, bf16[32,4096]{1,0:T(8,128)(2,1)} %collective-permute-done.10.refs_2_, ...), custom_call_target="tpu_custom_call" | custom-call | flops 8053063680 | bytes 4292608 | tf_op jit(solution)/shard_map/pallas_call | solution.py:124
  66.5 0.1 collective-permute-start.17
  66.6 0.4 collective-permute-start.16
  67.0 1.8 %collective-permute-start.15 = (bf16[32,4096]{1,0:T(8,128)(2,1)}, bf16[32,4096]{1,0:T(8,128)(2,1)S(1)}, u32[]{:S(2)}, u32[]{:S(2)}) collective-permute-start(bf16[32,4096]{1,0:T(8,128)(2,1)} %collective-permute-done.11.refs_3_), channel_id=1, source_target_pairs={{0,1},{1,0},{2,3},{3,2},{4,5},{5,4},{6,7},{7,6},{8,9},{9,8},{10,11... | collective-permute-start | bytes 786440 | tf_op jit(solution)/shard_map/ppermute | solution.py:35
  68.8 0.8 collective-permute-done.19.refs_8_
  69.5 1.7 %collective-permute-start.14 = (bf16[32,4096]{1,0:T(8,128)(2,1)}, bf16[32,4096]{1,0:T(8,128)(2,1)S(1)}, u32[]{:S(2)}, u32[]{:S(2)}) collective-permute-start(bf16[32,4096]{1,0:T(8,128)(2,1)} %collective-permute-done.10.refs_2_), channel_id=1, source_target_pairs={{0,1},{1,0},{2,3},{3,2},{4,5},{5,4},{6,7},{7,6},{8,9},{9,8},{10,11... | collective-permute-start | bytes 786440 | tf_op jit(solution)/shard_map/ppermute | solution.py:35
  71.2 2.0 %collective-permute-done.18.refs_7_ = bf16[32,4096]{1,0:T(8,128)(2,1)S(1)} collective-permute-done((bf16[32,4096]{1,0:T(8,128)(2,1)}, bf16[32,4096]{1,0:T(8,128)(2,1)S(1)}, u32[]{:S(2)}, u32[]{:S(2)}) %collective-permute-start.18) | collective-permute-done | bytes 262176 | tf_op jit(solution)/shard_map/ppermute | solution.py:35
  73.2 1.1 %collective-permute-start.13 = (bf16[32,4096]{1,0:T(8,128)(2,1)}, bf16[32,4096]{1,0:T(8,128)(2,1)S(1)}, u32[]{:S(2)}, u32[]{:S(2)}) collective-permute-start(bf16[32,4096]{1,0:T(8,128)(2,1)} %collective-permute-done.9.refs_1_), channel_id=1, source_target_pairs={{0,1},{1,0},{2,3},{3,2},{4,5},{5,4},{6,7},{7,6},{8,9},{9,8},{10,11... | collective-permute-start | bytes 786440 | tf_op jit(solution)/shard_map/ppermute | solution.py:35
  74.3 1.2 %collective-permute-start.12 = (bf16[32,4096]{1,0:T(8,128)(2,1)S(1)}, bf16[32,4096]{1,0:T(8,128)(2,1)S(1)}, u32[]{:S(2)}, u32[]{:S(2)}) collective-permute-start(bf16[32,4096]{1,0:T(8,128)(2,1)S(1)} %fusion.12.refs_0_), channel_id=1, source_target_pairs={{0,1},{1,0},{2,3},{3,2},{4,5},{5,4},{6,7},{7,6},{8,9},{9,8},{10,11... | collective-permute-start | bytes 786440 | tf_op jit(solution)/shard_map/ppermute | solution.py:35
  75.5 0.5 collective-permute-done.16.refs_5_
  76.0 1.1 %collective-permute-start.23 = (bf16[32,4096]{1,0:T(8,128)(2,1)S(1)}, bf16[32,4096]{1,0:T(8,128)(2,1)S(1)}, u32[]{:S(2)}, u32[]{:S(2)}) collective-permute-start(bf16[32,4096]{1,0:T(8,128)(2,1)S(1)} %collective-permute-done.19.refs_8_), channel_id=1, source_target_pairs={{0,1},{1,0},{2,3},{3,2},{4,5},{5,4},{6,7},{7,6},{8,9},{9,8},{10,11... | collective-permute-start | bytes 786440 | tf_op jit(solution)/shard_map/ppermute | solution.py:35
  77.1 0.0 collective-permute-start.22
  77.1 0.5 collective-permute-start.21
  77.6 0.1 collective-permute-start.20
  77.7 0.5 collective-permute-done.23.refs_12_
  78.2 0.4 collective-permute-done.22.refs_11_
  78.6 0.4 collective-permute-done.21.refs_10_
  79.0 0.4 collective-permute-done.20.refs_9_
  79.4 3.1 %shard_map.70 = bf16[512,384]{1,0:T(8,128)(2,1)} custom-call(s32[16]{0:T(128)S(1)} %stack.87.ids, bf16[4096,384]{1,0:T(8,128)(2,1)S(1)} %bitcast.36, bf16[512,384]{1,0:T(8,128)(2,1)} %get-tuple-element.28.refs_0_, bf16[32,4096]{1,0:T(8,128)(2,1)S(1)} %collective-permute-done.12.refs_1_, ...), custom_call_target="tpu_custom_call", output_to_operand_aliasing={{}: (2, {})} | custom-call | flops 1207959552 | bytes 6586368 | tf_op jit(solution)/shard_map/pallas_call | solution.py:124
  (16 shorter events, 0.0 us)
Async XLA Ops:
  0.8 1.2 %copy-start.1 = (bf16[1,512,896]{2,1,0:T(8,128)(2,1)S(1)}, bf16[1,512,896]{2,1,0:T(8,128)(2,1)}, u32[]{:S(2)}) copy-start(bf16[1,512,896]{2,1,0:T(8,128)(2,1)} %param.5) | copy-start | bytes 2752516
  2.0 7.5 %slice-start = ((s8[7340032]{0:T(1024)(128)(4,1)}), s8[4194304]{0:T(1024)(128)(4,1)S(1)}, s32[]{:S(2)}) async-start(s8[7340032]{0:T(1024)(128)(4,1)} %bitcast.41), calls=%async_computation | async-start | bytes 8388608
  2.6 6.8 %slice-start.1 = ((s8[7340032]{0:T(1024)(128)(4,1)}), s8[3145728]{0:T(1024)(128)(4,1)S(1)}, s32[]{:S(2)}) async-start(s8[7340032]{0:T(1024)(128)(4,1)} %bitcast.41), calls=%async_computation.1 | async-start | bytes 6291456
  8.5 3.2 %collective-permute-start.1 = (bf16[128,4096]{1,0:T(8,128)(2,1)S(1)}, bf16[128,4096]{1,0:T(8,128)(2,1)S(1)}, u32[]{:S(2)}, u32[]{:S(2)}) collective-permute-start(bf16[128,4096]{1,0:T(8,128)(2,1)S(1)} %get-tuple-element.41), channel_id=1, source_target_pairs={{0,1},{1,0},{2,3},{3,2},{4,5},{5,4},{6,7},{7,6},{8,9},{9,8},{10,11... | collective-permute-start | bytes 3145736 | tf_op jit(solution)/shard_map/ppermute | solution.py:35
  9.3 6.9 %collective-permute-start = (bf16[128,4096]{1,0:T(8,128)(2,1)S(1)}, bf16[128,4096]{1,0:T(8,128)(2,1)S(1)}, u32[]{:S(2)}, u32[]{:S(2)}) collective-permute-start(bf16[128,4096]{1,0:T(8,128)(2,1)S(1)} %get-tuple-element.40), channel_id=1, source_target_pairs={{0,1},{1,0},{2,3},{3,2},{4,5},{5,4},{6,7},{7,6},{8,9},{9,8},{10,11... | collective-permute-start | bytes 3145736 | tf_op jit(solution)/shard_map/ppermute | solution.py:35
  11.9 20.5 %copy-start.2 = (bf16[1,32,4096]{2,1,0:T(8,128)(2,1)S(1)}, bf16[1,32,4096]{2,1,0:T(8,128)(2,1)}, u32[]{:S(2)}) copy-start(bf16[1,32,4096]{2,1,0:T(8,128)(2,1)} %param.6) | copy-start | bytes 786436
  11.9 7.6 %collective-permute-start.3 = (bf16[32,4096]{1,0:T(8,128)(2,1)S(1)}, bf16[32,4096]{1,0:T(8,128)(2,1)S(1)}, u32[]{:S(2)}, u32[]{:S(2)}) collective-permute-start(bf16[32,4096]{1,0:T(8,128)(2,1)S(1)} %get-tuple-element.38), channel_id=1, source_target_pairs={{0,2},{1,3},{2,0},{3,1},{4,6},{5,7},{6,4},{7,5},{8,10},{9,11},{10,... | collective-permute-start | bytes 786440 | tf_op jit(solution)/shard_map/ppermute | solution.py:35
  12.1 10.3 %collective-permute-start.2 = (bf16[64,4096]{1,0:T(8,128)(2,1)S(1)}, bf16[64,4096]{1,0:T(8,128)(2,1)S(1)}, u32[]{:S(2)}, u32[]{:S(2)}) collective-permute-start(bf16[64,4096]{1,0:T(8,128)(2,1)S(1)} %add_convert_fusion), channel_id=1, source_target_pairs={{0,4},{1,13},{2,6},{3,15},{4,0},{5,9},{6,2},{7,11},{8,12},{9,5},{1... | collective-permute-start | bytes 1572872 | tf_op jit(solution)/shard_map/ppermute | solution.py:35
  14.7 10.4 %collective-permute-start.6 = (bf16[32,4096]{1,0:T(8,128)(2,1)S(1)}, bf16[32,4096]{1,0:T(8,128)(2,1)S(1)}, u32[]{:S(2)}, u32[]{:S(2)}) collective-permute-start(bf16[32,4096]{1,0:T(8,128)(2,1)S(1)} %get-tuple-element.39), channel_id=1, source_target_pairs={{0,2},{1,3},{2,0},{3,1},{4,6},{5,7},{6,4},{7,5},{8,10},{9,11},{10,... | collective-permute-start | bytes 786440 | tf_op jit(solution)/shard_map/ppermute | solution.py:35
  19.6 29.3 %copy-start.4 = (f32[1,4096]{1,0:T(1,128)S(1)}, f32[1,4096]{1,0:T(1,128)}, u32[]{:S(2)}) copy-start(f32[1,4096]{1,0:T(1,128)} %param.7) | copy-start | bytes 49156
  19.6 7.3 %collective-permute-start.4 = (bf16[32,4096]{1,0:T(8,128)(2,1)S(1)}, bf16[32,4096]{1,0:T(8,128)(2,1)S(1)}, u32[]{:S(2)}, u32[]{:S(2)}) collective-permute-start(bf16[32,4096]{1,0:T(8,128)(2,1)S(1)} %add_convert_fusion.4), channel_id=1, source_target_pairs={{0,8},{1,9},{2,10},{3,11},{4,12},{5,13},{6,14},{7,15},{8,0},{9,1},... | collective-permute-start | bytes 786440 | tf_op jit(solution)/shard_map/ppermute | solution.py:35
  22.5 40.9 %copy-start = (bf16[1,4096,384]{2,1,0:T(8,128)(2,1)S(1)}, bf16[1,4096,384]{2,1,0:T(8,128)(2,1)}, u32[]{:S(2)}) copy-start(bf16[1,4096,384]{2,1,0:T(8,128)(2,1)} %param.9) | copy-start | bytes 9437188
  25.2 7.2 %collective-permute-start.7 = (bf16[32,4096]{1,0:T(8,128)(2,1)S(1)}, bf16[32,4096]{1,0:T(8,128)(2,1)S(1)}, u32[]{:S(2)}, u32[]{:S(2)}) collective-permute-start(bf16[32,4096]{1,0:T(8,128)(2,1)S(1)} %add_convert_fusion.1), channel_id=1, source_target_pairs={{0,12},{1,5},{2,14},{3,7},{4,8},{5,1},{6,10},{7,3},{8,4},{9,13},{1... | collective-permute-start | bytes 786440 | tf_op jit(solution)/shard_map/ppermute | solution.py:35
  26.5 5.9 %collective-permute-start.5 = (bf16[32,4096]{1,0:T(8,128)(2,1)S(1)}, bf16[32,4096]{1,0:T(8,128)(2,1)S(1)}, u32[]{:S(2)}, u32[]{:S(2)}) collective-permute-start(bf16[32,4096]{1,0:T(8,128)(2,1)S(1)} %add_convert_fusion.3), channel_id=1, source_target_pairs={{0,2},{1,3},{2,0},{3,1},{4,6},{5,7},{6,4},{7,5},{8,10},{9,11},{10,... | collective-permute-start | bytes 786440 | tf_op jit(solution)/shard_map/ppermute | solution.py:35
  32.6 18.6 %copy-start.3 = (bf16[32,4096]{1,0:T(8,128)(2,1)}, bf16[32,4096]{1,0:T(8,128)(2,1)S(1)}, u32[]{:S(2)}) copy-start(bf16[32,4096]{1,0:T(8,128)(2,1)S(1)} %fusion.18) | copy-start | bytes 786436
  32.7 16.1 %collective-permute-start.8 = (bf16[32,4096]{1,0:T(8,128)(2,1)S(1)}, bf16[32,4096]{1,0:T(8,128)(2,1)S(1)}, u32[]{:S(2)}, u32[]{:S(2)}) collective-permute-start(bf16[32,4096]{1,0:T(8,128)(2,1)S(1)} %fusion.18), channel_id=1, source_target_pairs={{0,16},{16,32},{32,48},{48,0},{1,17},{17,33},{33,49},{49,1},{2,18}... | collective-permute-start | bytes 786440 | tf_op jit(solution)/shard_map/ppermute | solution.py:40
  49.0 6.1 %collective-permute-start.10 = (bf16[32,4096]{1,0:T(8,128)(2,1)S(1)}, bf16[32,4096]{1,0:T(8,128)(2,1)}, u32[]{:S(2)}, u32[]{:S(2)}) collective-permute-start(bf16[32,4096]{1,0:T(8,128)(2,1)S(1)} %fusion.12.refs_0_), channel_id=1, source_target_pairs={{0,12},{1,5},{2,14},{3,7},{4,8},{5,1},{6,10},{7,3},{8,4},{9,13},{1... | collective-permute-start | bytes 786440 | tf_op jit(solution)/shard_map/ppermute | solution.py:35
  51.3 5.6 %collective-permute-start.11 = (bf16[32,4096]{1,0:T(8,128)(2,1)S(1)}, bf16[32,4096]{1,0:T(8,128)(2,1)}, u32[]{:S(2)}, u32[]{:S(2)}) collective-permute-start(bf16[32,4096]{1,0:T(8,128)(2,1)S(1)} %fusion.12.refs_0_), channel_id=1, source_target_pairs={{0,2},{1,3},{2,0},{3,1},{4,6},{5,7},{6,4},{7,5},{8,10},{9,11},{10,... | collective-permute-start | bytes 786440 | tf_op jit(solution)/shard_map/ppermute | solution.py:35
  51.3 9.3 %collective-permute-start.9 = (bf16[32,4096]{1,0:T(8,128)(2,1)S(1)}, bf16[32,4096]{1,0:T(8,128)(2,1)}, u32[]{:S(2)}, u32[]{:S(2)}) collective-permute-start(bf16[32,4096]{1,0:T(8,128)(2,1)S(1)} %fusion.12.refs_0_), channel_id=1, source_target_pairs={{0,4},{1,13},{2,6},{3,15},{4,0},{5,9},{6,2},{7,11},{8,12},{9,5},{1... | collective-permute-start | bytes 786440 | tf_op jit(solution)/shard_map/ppermute | solution.py:35
  60.6 8.9 %collective-permute-start.19 = (bf16[32,4096]{1,0:T(8,128)(2,1)}, bf16[32,4096]{1,0:T(8,128)(2,1)S(1)}, u32[]{:S(2)}, u32[]{:S(2)}) collective-permute-start(bf16[32,4096]{1,0:T(8,128)(2,1)} %collective-permute-done.11.refs_3_), channel_id=1, source_target_pairs={{0,8},{1,9},{2,10},{3,11},{4,12},{5,13},{6,14},{7,15},{8,0},{9,1},... | collective-permute-start | bytes 786440 | tf_op jit(solution)/shard_map/ppermute | solution.py:35
  61.0 12.2 %collective-permute-start.18 = (bf16[32,4096]{1,0:T(8,128)(2,1)}, bf16[32,4096]{1,0:T(8,128)(2,1)S(1)}, u32[]{:S(2)}, u32[]{:S(2)}) collective-permute-start(bf16[32,4096]{1,0:T(8,128)(2,1)} %collective-permute-done.11.refs_3_), channel_id=1, source_target_pairs={{0,4},{1,13},{2,6},{3,15},{4,0},{5,9},{6,2},{7,11},{8,12},{9,5},{1... | collective-permute-start | bytes 786440 | tf_op jit(solution)/shard_map/ppermute | solution.py:35
  66.5 7.8 %collective-permute-start.17 = (bf16[32,4096]{1,0:T(8,128)(2,1)}, bf16[32,4096]{1,0:T(8,128)(2,1)S(1)}, u32[]{:S(2)}, u32[]{:S(2)}) collective-permute-start(bf16[32,4096]{1,0:T(8,128)(2,1)} %collective-permute-done.10.refs_2_), channel_id=1, source_target_pairs={{0,2},{1,3},{2,0},{3,1},{4,6},{5,7},{6,4},{7,5},{8,10},{9,11},{10,... | collective-permute-start | bytes 786440 | tf_op jit(solution)/shard_map/ppermute | solution.py:35
  66.6 9.4 %collective-permute-start.16 = (bf16[32,4096]{1,0:T(8,128)(2,1)}, bf16[32,4096]{1,0:T(8,128)(2,1)S(1)}, u32[]{:S(2)}, u32[]{:S(2)}) collective-permute-start(bf16[32,4096]{1,0:T(8,128)(2,1)} %collective-permute-done.10.refs_2_), channel_id=1, source_target_pairs={{0,4},{1,13},{2,6},{3,15},{4,0},{5,9},{6,2},{7,11},{8,12},{9,5},{1... | collective-permute-start | bytes 786440 | tf_op jit(solution)/shard_map/ppermute | solution.py:35
  67.0 10.1 %collective-permute-start.15 = (bf16[32,4096]{1,0:T(8,128)(2,1)}, bf16[32,4096]{1,0:T(8,128)(2,1)S(1)}, u32[]{:S(2)}, u32[]{:S(2)}) collective-permute-start(bf16[32,4096]{1,0:T(8,128)(2,1)} %collective-permute-done.11.refs_3_), channel_id=1, source_target_pairs={{0,1},{1,0},{2,3},{3,2},{4,5},{5,4},{6,7},{7,6},{8,9},{9,8},{10,11... | collective-permute-start | bytes 786440 | tf_op jit(solution)/shard_map/ppermute | solution.py:35
  69.5 7.6 %collective-permute-start.14 = (bf16[32,4096]{1,0:T(8,128)(2,1)}, bf16[32,4096]{1,0:T(8,128)(2,1)S(1)}, u32[]{:S(2)}, u32[]{:S(2)}) collective-permute-start(bf16[32,4096]{1,0:T(8,128)(2,1)} %collective-permute-done.10.refs_2_), channel_id=1, source_target_pairs={{0,1},{1,0},{2,3},{3,2},{4,5},{5,4},{6,7},{7,6},{8,9},{9,8},{10,11... | collective-permute-start | bytes 786440 | tf_op jit(solution)/shard_map/ppermute | solution.py:35
  73.2 4.4 %collective-permute-start.13 = (bf16[32,4096]{1,0:T(8,128)(2,1)}, bf16[32,4096]{1,0:T(8,128)(2,1)S(1)}, u32[]{:S(2)}, u32[]{:S(2)}) collective-permute-start(bf16[32,4096]{1,0:T(8,128)(2,1)} %collective-permute-done.9.refs_1_), channel_id=1, source_target_pairs={{0,1},{1,0},{2,3},{3,2},{4,5},{5,4},{6,7},{7,6},{8,9},{9,8},{10,11... | collective-permute-start | bytes 786440 | tf_op jit(solution)/shard_map/ppermute | solution.py:35
  74.3 3.4 %collective-permute-start.12 = (bf16[32,4096]{1,0:T(8,128)(2,1)S(1)}, bf16[32,4096]{1,0:T(8,128)(2,1)S(1)}, u32[]{:S(2)}, u32[]{:S(2)}) collective-permute-start(bf16[32,4096]{1,0:T(8,128)(2,1)S(1)} %fusion.12.refs_0_), channel_id=1, source_target_pairs={{0,1},{1,0},{2,3},{3,2},{4,5},{5,4},{6,7},{7,6},{8,9},{9,8},{10,11... | collective-permute-start | bytes 786440 | tf_op jit(solution)/shard_map/ppermute | solution.py:35
  76.0 2.2 %collective-permute-start.23 = (bf16[32,4096]{1,0:T(8,128)(2,1)S(1)}, bf16[32,4096]{1,0:T(8,128)(2,1)S(1)}, u32[]{:S(2)}, u32[]{:S(2)}) collective-permute-start(bf16[32,4096]{1,0:T(8,128)(2,1)S(1)} %collective-permute-done.19.refs_8_), channel_id=1, source_target_pairs={{0,1},{1,0},{2,3},{3,2},{4,5},{5,4},{6,7},{7,6},{8,9},{9,8},{10,11... | collective-permute-start | bytes 786440 | tf_op jit(solution)/shard_map/ppermute | solution.py:35
  77.1 1.5 %collective-permute-start.22 = (bf16[32,4096]{1,0:T(8,128)(2,1)S(1)}, bf16[32,4096]{1,0:T(8,128)(2,1)S(1)}, u32[]{:S(2)}, u32[]{:S(2)}) collective-permute-start(bf16[32,4096]{1,0:T(8,128)(2,1)S(1)} %collective-permute-done.18.refs_7_), channel_id=1, source_target_pairs={{0,1},{1,0},{2,3},{3,2},{4,5},{5,4},{6,7},{7,6},{8,9},{9,8},{10,11... | collective-permute-start | bytes 786440 | tf_op jit(solution)/shard_map/ppermute | solution.py:35
  77.1 1.9 %collective-permute-start.21 = (bf16[32,4096]{1,0:T(8,128)(2,1)S(1)}, bf16[32,4096]{1,0:T(8,128)(2,1)S(1)}, u32[]{:S(2)}, u32[]{:S(2)}) collective-permute-start(bf16[32,4096]{1,0:T(8,128)(2,1)S(1)} %collective-permute-done.17.refs_6_), channel_id=1, source_target_pairs={{0,1},{1,0},{2,3},{3,2},{4,5},{5,4},{6,7},{7,6},{8,9},{9,8},{10,11... | collective-permute-start | bytes 786440 | tf_op jit(solution)/shard_map/ppermute | solution.py:35
  77.6 1.8 %collective-permute-start.20 = (bf16[32,4096]{1,0:T(8,128)(2,1)S(1)}, bf16[32,4096]{1,0:T(8,128)(2,1)S(1)}, u32[]{:S(2)}, u32[]{:S(2)}) collective-permute-start(bf16[32,4096]{1,0:T(8,128)(2,1)S(1)} %collective-permute-done.16.refs_5_), channel_id=1, source_target_pairs={{0,1},{1,0},{2,3},{3,2},{4,5},{5,4},{6,7},{7,6},{8,9},{9,8},{10,11... | collective-permute-start | bytes 786440 | tf_op jit(solution)/shard_map/ppermute | solution.py:35

commit v4 on v3

--- a/solution.py
+++ b/solution.py
@@ -196,9 +196,9 @@
     near = [after(t, a, b, z) for t in (normed, a, b, z)]
     rows_near, ready = project(near, (0, 2, 3, 4), out_ids, qkv, weight=20)
     near_swap = [trade(after(t, ready), "core") for t in near]
-    late = [after(t, ready) for t in (ab, bz, az, abz)]
+    late = [after(t, ready) for t in (abz, bz, ab, az)]
     late_swap = [trade(t, "core") for t in late]
-    places = (8, 10, 11, 12, 1, 7, 5, 6, 9, 15, 13, 14)
+    places = (8, 10, 11, 12, 6, 7, 1, 5, 14, 15, 9, 13)
     (proj,) = project(near_swap + late + late_swap, places, out_ids, qkv, before=rows_near)
     return (out[None], proj[None])
 

time: 83.3 us -> 85.2 us (1.023)
  waiting for transfers between devices: 36.1 us -> 39.2 us
  starting transfers between devices: 27.9 us -> 26.5 us
    ppermute x23, waiting for transfers between devices: 23.1 us -> 26.2 us  [trade(): return lax.ppermute(value, AXES, pairs)]
    ppermute x23, starting transfers between devices: 24.9 us -> 23.4 us  [trade(): return lax.ppermute(value, AXES, pairs)]
where the time goes in v4:
time: 85.2 us; the launch traced here: 84.3 us
  waiting for transfers between devices  39.2 us (46%)
  starting transfers between devices  26.5 us (31%)
  matrix products  8.06 us (9%)
  Pallas kernels  6.83 us (8%)
  local copies, waits for them, and re-layouts  1.61 us (2%)
  other arithmetic  1.09 us (1%)
  between operations  1.03 us (1%)
    ppermute x23, waiting for transfers between devices, trade(): return lax.ppermute(value, AXES, pairs)  26.2 us
    ppermute x23, starting transfers between devices, trade(): return lax.ppermute(value, AXES, pairs)  23.4 us
    ppermute x1, waiting for transfers between devices, next_section(): lax.ppermute(value, 'pipe', [(s, (s + 1) % count) for s in range(count)])  13 us
    dot_general x2, matrix products, dot_bf16(): jnp.dot(a, b, preferred_element_type=jnp.float32).astype(jnp.bfloat16)  8.06 us
    pallas_call x2, Pallas kernels, project(): pl.pallas_call(functools.partial(project_kernel, places, before is None),...  6.21 us
    ppermute x1, starting transfers between devices, next_section(): lax.ppermute(value, 'pipe', [(s, (s + 1) % count) for s in range(count)])  3.07 us
  transfers between devices with their start and end apart: 24, of which 15 were waited for; matrix products, arithmetic and copies ran while one was open for 4% of the time, Pallas kernels for 4%

profile of v4, /device:TPU:41, one launch (start us, length us, event | category | flops | bytes accessed | tf_op | source)
XLA Modules:
  0.0 84.3 jit_solution(8195327026665006720)
XLA Ops:
  0.7 0.1 stack.86.ids
  0.8 0.0 copy-start.1
  0.8 1.2 %copy-done.1 = bf16[1,512,896]{2,1,0:T(8,128)(2,1)S(1)} copy-done((bf16[1,512,896]{2,1,0:T(8,128)(2,1)S(1)}, bf16[1,512,896]{2,1,0:T(8,128)(2,1)}, u32[]{:S(2)}) %copy-start.1) | copy-done | bytes 917528
  2.0 0.6 shard_map.68
  2.6 0.0 slice-start.1
  2.6 5.7 %fusion.7 = bf16[256,4096]{1,0:T(8,128)(2,1)S(1)} fusion(bf16[256,896]{1,0:T(8,128)(2,1)S(1)} %get-tuple-element.21, bf16[1,896,4096]{2,1,0:T(8,128)(2,1)} %param.8), kind=kOutput, calls=%fused_computation.5 | convolution fusion | flops 1880096768 | bytes 9895936 | tf_op jit(solution)/shard_map/dot_general | solution.py:147
  8.3 0.2 fusion.19
  8.5 0.8 collective-permute-start.1
  9.3 0.1 collective-permute-start
  9.4 2.3 %fusion.4 = bf16[256,4096]{1,0:T(8,128)(2,1)S(1)} fusion(bf16[256,896]{1,0:T(8,128)(2,1)S(1)} %get-tuple-element.20, bf16[1,896,4096]{2,1,0:T(8,128)(2,1)S(1)} %bitcast.42), kind=kOutput, calls=%fused_computation.4 | convolution fusion | flops 1880096768 | bytes 9895936 | tf_op jit(solution)/shard_map/dot_general | solution.py:147
  11.8 0.0 collective-permute-done.1
  11.8 0.1 add_convert_fusion.5
  11.9 0.0 copy-start.2
  11.9 0.1 collective-permute-start.3
  12.0 0.1 add_convert_fusion
  12.1 2.6 %collective-permute-start.2 = (bf16[64,4096]{1,0:T(8,128)(2,1)S(1)}, bf16[64,4096]{1,0:T(8,128)(2,1)S(1)}, u32[]{:S(2)}, u32[]{:S(2)}) collective-permute-start(bf16[64,4096]{1,0:T(8,128)(2,1)S(1)} %add_convert_fusion), channel_id=1, source_target_pairs={{0,4},{1,13},{2,6},{3,15},{4,0},{5,9},{6,2},{7,11},{8,12},{9,5},{1... | collective-permute-start | bytes 1572872 | tf_op jit(solution)/shard_map/ppermute | solution.py:35
  14.7 1.4 %collective-permute-start.6 = (bf16[32,4096]{1,0:T(8,128)(2,1)S(1)}, bf16[32,4096]{1,0:T(8,128)(2,1)S(1)}, u32[]{:S(2)}, u32[]{:S(2)}) collective-permute-start(bf16[32,4096]{1,0:T(8,128)(2,1)S(1)} %get-tuple-element.39), channel_id=1, source_target_pairs={{0,2},{1,3},{2,0},{3,1},{4,6},{5,7},{6,4},{7,5},{8,10},{9,11},{10,... | collective-permute-start | bytes 786440 | tf_op jit(solution)/shard_map/ppermute | solution.py:35
  16.2 0.0 collective-permute-done
  16.2 3.3 %collective-permute-done.3 = bf16[32,4096]{1,0:T(8,128)(2,1)S(1)} collective-permute-done((bf16[32,4096]{1,0:T(8,128)(2,1)S(1)}, bf16[32,4096]{1,0:T(8,128)(2,1)S(1)}, u32[]{:S(2)}, u32[]{:S(2)}) %collective-permute-start.3) | collective-permute-done | bytes 262176 | tf_op jit(solution)/shard_map/ppermute | solution.py:35
  19.5 0.1 add_convert_fusion.4
  19.6 0.0 copy-start.4
  19.6 2.8 %collective-permute-start.4 = (bf16[32,4096]{1,0:T(8,128)(2,1)S(1)}, bf16[32,4096]{1,0:T(8,128)(2,1)S(1)}, u32[]{:S(2)}, u32[]{:S(2)}) collective-permute-start(bf16[32,4096]{1,0:T(8,128)(2,1)S(1)} %add_convert_fusion.4), channel_id=1, source_target_pairs={{0,8},{1,9},{2,10},{3,11},{4,12},{5,13},{6,14},{7,15},{8,0},{9,1},... | collective-permute-start | bytes 786440 | tf_op jit(solution)/shard_map/ppermute | solution.py:35
  22.4 0.1 add_convert_fusion.3
  22.5 0.0 copy-start
  22.5 2.6 %collective-permute-done.6 = bf16[32,4096]{1,0:T(8,128)(2,1)S(1)} collective-permute-done((bf16[32,4096]{1,0:T(8,128)(2,1)S(1)}, bf16[32,4096]{1,0:T(8,128)(2,1)S(1)}, u32[]{:S(2)}, u32[]{:S(2)}) %collective-permute-start.6) | collective-permute-done | bytes 262176 | tf_op jit(solution)/shard_map/ppermute | solution.py:35
  25.1 0.1 add_convert_fusion.1
  25.2 1.3 %collective-permute-start.7 = (bf16[32,4096]{1,0:T(8,128)(2,1)S(1)}, bf16[32,4096]{1,0:T(8,128)(2,1)S(1)}, u32[]{:S(2)}, u32[]{:S(2)}) collective-permute-start(bf16[32,4096]{1,0:T(8,128)(2,1)S(1)} %add_convert_fusion.1), channel_id=1, source_target_pairs={{0,12},{1,5},{2,14},{3,7},{4,8},{5,1},{6,10},{7,3},{8,4},{9,13},{1... | collective-permute-start | bytes 786440 | tf_op jit(solution)/shard_map/ppermute | solution.py:35
  26.5 0.2 collective-permute-start.5
  26.7 0.2 collective-permute-done.4
  26.9 5.5 %collective-permute-done.7 = bf16[32,4096]{1,0:T(8,128)(2,1)S(1)} collective-permute-done((bf16[32,4096]{1,0:T(8,128)(2,1)S(1)}, bf16[32,4096]{1,0:T(8,128)(2,1)S(1)}, u32[]{:S(2)}, u32[]{:S(2)}) %collective-permute-start.7) | collective-permute-done | bytes 262176 | tf_op jit(solution)/shard_map/ppermute | solution.py:35
  32.4 0.0 collective-permute-done.5
  32.4 0.2 fusion.18
  32.6 0.0 copy-start.3
  32.7 3.1 %collective-permute-start.8 = (bf16[32,4096]{1,0:T(8,128)(2,1)S(1)}, bf16[32,4096]{1,0:T(8,128)(2,1)S(1)}, u32[]{:S(2)}, u32[]{:S(2)}) collective-permute-start(bf16[32,4096]{1,0:T(8,128)(2,1)S(1)} %fusion.18), channel_id=1, source_target_pairs={{0,16},{16,32},{32,48},{48,0},{1,17},{17,33},{33,49},{49,1},{2,18}... | collective-permute-start | bytes 786440 | tf_op jit(solution)/shard_map/ppermute | solution.py:40
  35.7 13.0 %collective-permute-done.8 = bf16[32,4096]{1,0:T(8,128)(2,1)S(1)} collective-permute-done((bf16[32,4096]{1,0:T(8,128)(2,1)S(1)}, bf16[32,4096]{1,0:T(8,128)(2,1)S(1)}, u32[]{:S(2)}, u32[]{:S(2)}) %collective-permute-start.8) | collective-permute-done | bytes 262176 | tf_op jit(solution)/shard_map/ppermute | solution.py:40
  48.7 0.2 fusion.10
  48.9 0.1 fusion.12.refs_0_
  49.0 2.2 %collective-permute-start.10 = (bf16[32,4096]{1,0:T(8,128)(2,1)S(1)}, bf16[32,4096]{1,0:T(8,128)(2,1)}, u32[]{:S(2)}, u32[]{:S(2)}) collective-permute-start(bf16[32,4096]{1,0:T(8,128)(2,1)S(1)} %fusion.12.refs_0_), channel_id=1, source_target_pairs={{0,12},{1,5},{2,14},{3,7},{4,8},{5,1},{6,10},{7,3},{8,4},{9,13},{1... | collective-permute-start | bytes 786440 | tf_op jit(solution)/shard_map/ppermute | solution.py:35
  51.3 2.6 %collective-permute-start.9 = (bf16[32,4096]{1,0:T(8,128)(2,1)S(1)}, bf16[32,4096]{1,0:T(8,128)(2,1)}, u32[]{:S(2)}, u32[]{:S(2)}) collective-permute-start(bf16[32,4096]{1,0:T(8,128)(2,1)S(1)} %fusion.12.refs_0_), channel_id=1, source_target_pairs={{0,4},{1,13},{2,6},{3,15},{4,0},{5,9},{6,2},{7,11},{8,12},{9,5},{1... | collective-permute-start | bytes 786440 | tf_op jit(solution)/shard_map/ppermute | solution.py:35
  53.9 0.1 stack.87.ids
  54.0 1.1 %collective-permute-done.10.refs_2_ = bf16[32,4096]{1,0:T(8,128)(2,1)} collective-permute-done((bf16[32,4096]{1,0:T(8,128)(2,1)S(1)}, bf16[32,4096]{1,0:T(8,128)(2,1)}, u32[]{:S(2)}, u32[]{:S(2)}) %collective-permute-start.10) | collective-permute-done | bytes 262176 | tf_op jit(solution)/shard_map/ppermute | solution.py:35
  55.2 1.8 %collective-permute-done.11.refs_3_ = bf16[32,4096]{1,0:T(8,128)(2,1)} collective-permute-done((bf16[32,4096]{1,0:T(8,128)(2,1)S(1)}, bf16[32,4096]{1,0:T(8,128)(2,1)}, u32[]{:S(2)}, u32[]{:S(2)}) %collective-permute-start.11) | collective-permute-done | bytes 262176 | tf_op jit(solution)/shard_map/ppermute | solution.py:35
  56.9 3.7 %collective-permute-done.9.refs_1_ = bf16[32,4096]{1,0:T(8,128)(2,1)} collective-permute-done((bf16[32,4096]{1,0:T(8,128)(2,1)S(1)}, bf16[32,4096]{1,0:T(8,128)(2,1)}, u32[]{:S(2)}, u32[]{:S(2)}) %collective-permute-start.9) | collective-permute-done | bytes 262176 | tf_op jit(solution)/shard_map/ppermute | solution.py:35
  60.6 2.7 %collective-permute-start.19 = (bf16[32,4096]{1,0:T(8,128)(2,1)}, bf16[32,4096]{1,0:T(8,128)(2,1)S(1)}, u32[]{:S(2)}, u32[]{:S(2)}) collective-permute-start(bf16[32,4096]{1,0:T(8,128)(2,1)} %collective-permute-done.11.refs_3_), channel_id=1, source_target_pairs={{0,4},{1,13},{2,6},{3,15},{4,0},{5,9},{6,2},{7,11},{8,12},{9,5},{1... | collective-permute-start | bytes 786440 | tf_op jit(solution)/shard_map/ppermute | solution.py:35
  63.4 0.0 collective-permute-start.18
  63.4 3.1 %shard_map.69 = (bf16[512,384]{1,0:T(8,128)(2,1)}, f32[8,128]{1,0:T(8,128)}) custom-call(s32[16]{0:T(128)S(1)} %stack.87.ids, bf16[4096,384]{1,0:T(8,128)(2,1)S(1)} %bitcast.35, bf16[32,4096]{1,0:T(8,128)(2,1)S(1)} %fusion.12.refs_0_, bf16[32,4096]{1,0:T(8,128)(2,1)} %collective-permute-done.9.refs_1_, bf16[32,4096]{1,0:T(8,128)(2,1)} %collective-permute-done.10.refs_2_, ...), custom_call_target="tpu_custom_call" | custom-call | flops 8053063680 | bytes 4292608 | tf_op jit(solution)/shard_map/pallas_call | solution.py:124
  66.5 0.1 collective-permute-start.17
  66.6 0.1 collective-permute-start.16
  66.7 2.4 %collective-permute-start.15 = (bf16[32,4096]{1,0:T(8,128)(2,1)}, bf16[32,4096]{1,0:T(8,128)(2,1)S(1)}, u32[]{:S(2)}, u32[]{:S(2)}) collective-permute-start(bf16[32,4096]{1,0:T(8,128)(2,1)} %collective-permute-done.11.refs_3_), channel_id=1, source_target_pairs={{0,1},{1,0},{2,3},{3,2},{4,5},{5,4},{6,7},{7,6},{8,9},{9,8},{10,11... | collective-permute-start | bytes 786440 | tf_op jit(solution)/shard_map/ppermute | solution.py:35
  69.1 0.0 collective-permute-start.14
  69.1 1.0 %collective-permute-done.18.refs_7_ = bf16[32,4096]{1,0:T(8,128)(2,1)S(1)} collective-permute-done((bf16[32,4096]{1,0:T(8,128)(2,1)}, bf16[32,4096]{1,0:T(8,128)(2,1)S(1)}, u32[]{:S(2)}, u32[]{:S(2)}) %collective-permute-start.18) | collective-permute-done | bytes 262176 | tf_op jit(solution)/shard_map/ppermute | solution.py:35
  70.2 0.6 collective-permute-start.13
  70.7 4.0 %collective-permute-done.17.refs_6_ = bf16[32,4096]{1,0:T(8,128)(2,1)S(1)} collective-permute-done((bf16[32,4096]{1,0:T(8,128)(2,1)}, bf16[32,4096]{1,0:T(8,128)(2,1)S(1)}, u32[]{:S(2)}, u32[]{:S(2)}) %collective-permute-start.17) | collective-permute-done | bytes 262176 | tf_op jit(solution)/shard_map/ppermute | solution.py:35
  74.8 0.7 collective-permute-start.12
  75.5 1.3 %collective-permute-done.16.refs_5_ = bf16[32,4096]{1,0:T(8,128)(2,1)S(1)} collective-permute-done((bf16[32,4096]{1,0:T(8,128)(2,1)}, bf16[32,4096]{1,0:T(8,128)(2,1)S(1)}, u32[]{:S(2)}, u32[]{:S(2)}) %collective-permute-start.16) | collective-permute-done | bytes 262176 | tf_op jit(solution)/shard_map/ppermute | solution.py:35
  76.8 1.9 %collective-permute-start.23 = (bf16[32,4096]{1,0:T(8,128)(2,1)S(1)}, bf16[32,4096]{1,0:T(8,128)(2,1)S(1)}, u32[]{:S(2)}, u32[]{:S(2)}) collective-permute-start(bf16[32,4096]{1,0:T(8,128)(2,1)S(1)} %collective-permute-done.19.refs_8_), channel_id=1, source_target_pairs={{0,1},{1,0},{2,3},{3,2},{4,5},{5,4},{6,7},{7,6},{8,9},{9,8},{10,11... | collective-permute-start | bytes 786440 | tf_op jit(solution)/shard_map/ppermute | solution.py:35
  78.7 0.0 collective-permute-start.22
  78.7 0.5 collective-permute-start.21
  79.2 0.1 collective-permute-start.20
  79.3 0.5 collective-permute-done.23.refs_12_
  79.9 0.4 collective-permute-done.22.refs_11_
  80.2 0.4 collective-permute-done.21.refs_10_
  80.6 0.4 collective-permute-done.20.refs_9_
  81.0 3.1 %shard_map.70 = bf16[512,384]{1,0:T(8,128)(2,1)} custom-call(s32[16]{0:T(128)S(1)} %stack.87.ids, bf16[4096,384]{1,0:T(8,128)(2,1)S(1)} %bitcast.36, bf16[512,384]{1,0:T(8,128)(2,1)} %get-tuple-element.28.refs_0_, bf16[32,4096]{1,0:T(8,128)(2,1)S(1)} %collective-permute-done.12.refs_1_, ...), custom_call_target="tpu_custom_call", output_to_operand_aliasing={{}: (2, {})} | custom-call | flops 1207959552 | bytes 6586368 | tf_op jit(solution)/shard_map/pallas_call | solution.py:124
  (16 shorter events, 0.0 us)
Async XLA Ops:
  0.8 1.2 %copy-start.1 = (bf16[1,512,896]{2,1,0:T(8,128)(2,1)S(1)}, bf16[1,512,896]{2,1,0:T(8,128)(2,1)}, u32[]{:S(2)}) copy-start(bf16[1,512,896]{2,1,0:T(8,128)(2,1)} %param.5) | copy-start | bytes 2752516
  2.0 7.5 %slice-start = ((s8[7340032]{0:T(1024)(128)(4,1)}), s8[4194304]{0:T(1024)(128)(4,1)S(1)}, s32[]{:S(2)}) async-start(s8[7340032]{0:T(1024)(128)(4,1)} %bitcast.41), calls=%async_computation | async-start | bytes 8388608
  2.6 6.8 %slice-start.1 = ((s8[7340032]{0:T(1024)(128)(4,1)}), s8[3145728]{0:T(1024)(128)(4,1)S(1)}, s32[]{:S(2)}) async-start(s8[7340032]{0:T(1024)(128)(4,1)} %bitcast.41), calls=%async_computation.1 | async-start | bytes 6291456
  8.5 3.2 %collective-permute-start.1 = (bf16[128,4096]{1,0:T(8,128)(2,1)S(1)}, bf16[128,4096]{1,0:T(8,128)(2,1)S(1)}, u32[]{:S(2)}, u32[]{:S(2)}) collective-permute-start(bf16[128,4096]{1,0:T(8,128)(2,1)S(1)} %get-tuple-element.41), channel_id=1, source_target_pairs={{0,1},{1,0},{2,3},{3,2},{4,5},{5,4},{6,7},{7,6},{8,9},{9,8},{10,11... | collective-permute-start | bytes 3145736 | tf_op jit(solution)/shard_map/ppermute | solution.py:35
  9.3 6.9 %collective-permute-start = (bf16[128,4096]{1,0:T(8,128)(2,1)S(1)}, bf16[128,4096]{1,0:T(8,128)(2,1)S(1)}, u32[]{:S(2)}, u32[]{:S(2)}) collective-permute-start(bf16[128,4096]{1,0:T(8,128)(2,1)S(1)} %get-tuple-element.40), channel_id=1, source_target_pairs={{0,1},{1,0},{2,3},{3,2},{4,5},{5,4},{6,7},{7,6},{8,9},{9,8},{10,11... | collective-permute-start | bytes 3145736 | tf_op jit(solution)/shard_map/ppermute | solution.py:35
  11.9 20.5 %copy-start.2 = (bf16[1,32,4096]{2,1,0:T(8,128)(2,1)S(1)}, bf16[1,32,4096]{2,1,0:T(8,128)(2,1)}, u32[]{:S(2)}) copy-start(bf16[1,32,4096]{2,1,0:T(8,128)(2,1)} %param.6) | copy-start | bytes 786436
  11.9 7.6 %collective-permute-start.3 = (bf16[32,4096]{1,0:T(8,128)(2,1)S(1)}, bf16[32,4096]{1,0:T(8,128)(2,1)S(1)}, u32[]{:S(2)}, u32[]{:S(2)}) collective-permute-start(bf16[32,4096]{1,0:T(8,128)(2,1)S(1)} %get-tuple-element.38), channel_id=1, source_target_pairs={{0,2},{1,3},{2,0},{3,1},{4,6},{5,7},{6,4},{7,5},{8,10},{9,11},{10,... | collective-permute-start | bytes 786440 | tf_op jit(solution)/shard_map/ppermute | solution.py:35
  12.1 10.3 %collective-permute-start.2 = (bf16[64,4096]{1,0:T(8,128)(2,1)S(1)}, bf16[64,4096]{1,0:T(8,128)(2,1)S(1)}, u32[]{:S(2)}, u32[]{:S(2)}) collective-permute-start(bf16[64,4096]{1,0:T(8,128)(2,1)S(1)} %add_convert_fusion), channel_id=1, source_target_pairs={{0,4},{1,13},{2,6},{3,15},{4,0},{5,9},{6,2},{7,11},{8,12},{9,5},{1... | collective-permute-start | bytes 1572872 | tf_op jit(solution)/shard_map/ppermute | solution.py:35
  14.7 10.4 %collective-permute-start.6 = (bf16[32,4096]{1,0:T(8,128)(2,1)S(1)}, bf16[32,4096]{1,0:T(8,128)(2,1)S(1)}, u32[]{:S(2)}, u32[]{:S(2)}) collective-permute-start(bf16[32,4096]{1,0:T(8,128)(2,1)S(1)} %get-tuple-element.39), channel_id=1, source_target_pairs={{0,2},{1,3},{2,0},{3,1},{4,6},{5,7},{6,4},{7,5},{8,10},{9,11},{10,... | collective-permute-start | bytes 786440 | tf_op jit(solution)/shard_map/ppermute | solution.py:35
  19.6 29.3 %copy-start.4 = (f32[1,4096]{1,0:T(1,128)S(1)}, f32[1,4096]{1,0:T(1,128)}, u32[]{:S(2)}) copy-start(f32[1,4096]{1,0:T(1,128)} %param.7) | copy-start | bytes 49156
  19.6 7.3 %collective-permute-start.4 = (bf16[32,4096]{1,0:T(8,128)(2,1)S(1)}, bf16[32,4096]{1,0:T(8,128)(2,1)S(1)}, u32[]{:S(2)}, u32[]{:S(2)}) collective-permute-start(bf16[32,4096]{1,0:T(8,128)(2,1)S(1)} %add_convert_fusion.4), channel_id=1, source_target_pairs={{0,8},{1,9},{2,10},{3,11},{4,12},{5,13},{6,14},{7,15},{8,0},{9,1},... | collective-permute-start | bytes 786440 | tf_op jit(solution)/shard_map/ppermute | solution.py:35
  22.5 40.9 %copy-start = (bf16[1,4096,384]{2,1,0:T(8,128)(2,1)S(1)}, bf16[1,4096,384]{2,1,0:T(8,128)(2,1)}, u32[]{:S(2)}) copy-start(bf16[1,4096,384]{2,1,0:T(8,128)(2,1)} %param.9) | copy-start | bytes 9437188
  25.2 7.2 %collective-permute-start.7 = (bf16[32,4096]{1,0:T(8,128)(2,1)S(1)}, bf16[32,4096]{1,0:T(8,128)(2,1)S(1)}, u32[]{:S(2)}, u32[]{:S(2)}) collective-permute-start(bf16[32,4096]{1,0:T(8,128)(2,1)S(1)} %add_convert_fusion.1), channel_id=1, source_target_pairs={{0,12},{1,5},{2,14},{3,7},{4,8},{5,1},{6,10},{7,3},{8,4},{9,13},{1... | collective-permute-start | bytes 786440 | tf_op jit(solution)/shard_map/ppermute | solution.py:35
  26.5 5.9 %collective-permute-start.5 = (bf16[32,4096]{1,0:T(8,128)(2,1)S(1)}, bf16[32,4096]{1,0:T(8,128)(2,1)S(1)}, u32[]{:S(2)}, u32[]{:S(2)}) collective-permute-start(bf16[32,4096]{1,0:T(8,128)(2,1)S(1)} %add_convert_fusion.3), channel_id=1, source_target_pairs={{0,2},{1,3},{2,0},{3,1},{4,6},{5,7},{6,4},{7,5},{8,10},{9,11},{10,... | collective-permute-start | bytes 786440 | tf_op jit(solution)/shard_map/ppermute | solution.py:35
  32.6 18.6 %copy-start.3 = (bf16[32,4096]{1,0:T(8,128)(2,1)}, bf16[32,4096]{1,0:T(8,128)(2,1)S(1)}, u32[]{:S(2)}) copy-start(bf16[32,4096]{1,0:T(8,128)(2,1)S(1)} %fusion.18) | copy-start | bytes 786436
  32.7 16.1 %collective-permute-start.8 = (bf16[32,4096]{1,0:T(8,128)(2,1)S(1)}, bf16[32,4096]{1,0:T(8,128)(2,1)S(1)}, u32[]{:S(2)}, u32[]{:S(2)}) collective-permute-start(bf16[32,4096]{1,0:T(8,128)(2,1)S(1)} %fusion.18), channel_id=1, source_target_pairs={{0,16},{16,32},{32,48},{48,0},{1,17},{17,33},{33,49},{49,1},{2,18}... | collective-permute-start | bytes 786440 | tf_op jit(solution)/shard_map/ppermute | solution.py:40
  49.0 6.1 %collective-permute-start.10 = (bf16[32,4096]{1,0:T(8,128)(2,1)S(1)}, bf16[32,4096]{1,0:T(8,128)(2,1)}, u32[]{:S(2)}, u32[]{:S(2)}) collective-permute-start(bf16[32,4096]{1,0:T(8,128)(2,1)S(1)} %fusion.12.refs_0_), channel_id=1, source_target_pairs={{0,12},{1,5},{2,14},{3,7},{4,8},{5,1},{6,10},{7,3},{8,4},{9,13},{1... | collective-permute-start | bytes 786440 | tf_op jit(solution)/shard_map/ppermute | solution.py:35
  51.3 5.6 %collective-permute-start.11 = (bf16[32,4096]{1,0:T(8,128)(2,1)S(1)}, bf16[32,4096]{1,0:T(8,128)(2,1)}, u32[]{:S(2)}, u32[]{:S(2)}) collective-permute-start(bf16[32,4096]{1,0:T(8,128)(2,1)S(1)} %fusion.12.refs_0_), channel_id=1, source_target_pairs={{0,2},{1,3},{2,0},{3,1},{4,6},{5,7},{6,4},{7,5},{8,10},{9,11},{10,... | collective-permute-start | bytes 786440 | tf_op jit(solution)/shard_map/ppermute | solution.py:35
  51.3 9.3 %collective-permute-start.9 = (bf16[32,4096]{1,0:T(8,128)(2,1)S(1)}, bf16[32,4096]{1,0:T(8,128)(2,1)}, u32[]{:S(2)}, u32[]{:S(2)}) collective-permute-start(bf16[32,4096]{1,0:T(8,128)(2,1)S(1)} %fusion.12.refs_0_), channel_id=1, source_target_pairs={{0,4},{1,13},{2,6},{3,15},{4,0},{5,9},{6,2},{7,11},{8,12},{9,5},{1... | collective-permute-start | bytes 786440 | tf_op jit(solution)/shard_map/ppermute | solution.py:35
  60.6 8.5 %collective-permute-start.19 = (bf16[32,4096]{1,0:T(8,128)(2,1)}, bf16[32,4096]{1,0:T(8,128)(2,1)S(1)}, u32[]{:S(2)}, u32[]{:S(2)}) collective-permute-start(bf16[32,4096]{1,0:T(8,128)(2,1)} %collective-permute-done.11.refs_3_), channel_id=1, source_target_pairs={{0,4},{1,13},{2,6},{3,15},{4,0},{5,9},{6,2},{7,11},{8,12},{9,5},{1... | collective-permute-start | bytes 786440 | tf_op jit(solution)/shard_map/ppermute | solution.py:35
  63.4 6.8 %collective-permute-start.18 = (bf16[32,4096]{1,0:T(8,128)(2,1)}, bf16[32,4096]{1,0:T(8,128)(2,1)S(1)}, u32[]{:S(2)}, u32[]{:S(2)}) collective-permute-start(bf16[32,4096]{1,0:T(8,128)(2,1)} %collective-permute-done.10.refs_2_), channel_id=1, source_target_pairs={{0,4},{1,13},{2,6},{3,15},{4,0},{5,9},{6,2},{7,11},{8,12},{9,5},{1... | collective-permute-start | bytes 786440 | tf_op jit(solution)/shard_map/ppermute | solution.py:35
  66.5 8.3 %collective-permute-start.17 = (bf16[32,4096]{1,0:T(8,128)(2,1)}, bf16[32,4096]{1,0:T(8,128)(2,1)S(1)}, u32[]{:S(2)}, u32[]{:S(2)}) collective-permute-start(bf16[32,4096]{1,0:T(8,128)(2,1)} %collective-permute-done.10.refs_2_), channel_id=1, source_target_pairs={{0,2},{1,3},{2,0},{3,1},{4,6},{5,7},{6,4},{7,5},{8,10},{9,11},{10,... | collective-permute-start | bytes 786440 | tf_op jit(solution)/shard_map/ppermute | solution.py:35
  66.6 10.2 %collective-permute-start.16 = (bf16[32,4096]{1,0:T(8,128)(2,1)}, bf16[32,4096]{1,0:T(8,128)(2,1)S(1)}, u32[]{:S(2)}, u32[]{:S(2)}) collective-permute-start(bf16[32,4096]{1,0:T(8,128)(2,1)} %collective-permute-done.11.refs_3_), channel_id=1, source_target_pairs={{0,8},{1,9},{2,10},{3,11},{4,12},{5,13},{6,14},{7,15},{8,0},{9,1},... | collective-permute-start | bytes 786440 | tf_op jit(solution)/shard_map/ppermute | solution.py:35
  66.7 12.0 %collective-permute-start.15 = (bf16[32,4096]{1,0:T(8,128)(2,1)}, bf16[32,4096]{1,0:T(8,128)(2,1)S(1)}, u32[]{:S(2)}, u32[]{:S(2)}) collective-permute-start(bf16[32,4096]{1,0:T(8,128)(2,1)} %collective-permute-done.11.refs_3_), channel_id=1, source_target_pairs={{0,1},{1,0},{2,3},{3,2},{4,5},{5,4},{6,7},{7,6},{8,9},{9,8},{10,11... | collective-permute-start | bytes 786440 | tf_op jit(solution)/shard_map/ppermute | solution.py:35
  69.1 9.6 %collective-permute-start.14 = (bf16[32,4096]{1,0:T(8,128)(2,1)}, bf16[32,4096]{1,0:T(8,128)(2,1)S(1)}, u32[]{:S(2)}, u32[]{:S(2)}) collective-permute-start(bf16[32,4096]{1,0:T(8,128)(2,1)} %collective-permute-done.10.refs_2_), channel_id=1, source_target_pairs={{0,1},{1,0},{2,3},{3,2},{4,5},{5,4},{6,7},{7,6},{8,9},{9,8},{10,11... | collective-permute-start | bytes 786440 | tf_op jit(solution)/shard_map/ppermute | solution.py:35
  70.2 9.1 %collective-permute-start.13 = (bf16[32,4096]{1,0:T(8,128)(2,1)}, bf16[32,4096]{1,0:T(8,128)(2,1)S(1)}, u32[]{:S(2)}, u32[]{:S(2)}) collective-permute-start(bf16[32,4096]{1,0:T(8,128)(2,1)} %collective-permute-done.9.refs_1_), channel_id=1, source_target_pairs={{0,1},{1,0},{2,3},{3,2},{4,5},{5,4},{6,7},{7,6},{8,9},{9,8},{10,11... | collective-permute-start | bytes 786440 | tf_op jit(solution)/shard_map/ppermute | solution.py:35
  74.8 4.5 %collective-permute-start.12 = (bf16[32,4096]{1,0:T(8,128)(2,1)S(1)}, bf16[32,4096]{1,0:T(8,128)(2,1)S(1)}, u32[]{:S(2)}, u32[]{:S(2)}) collective-permute-start(bf16[32,4096]{1,0:T(8,128)(2,1)S(1)} %fusion.12.refs_0_), channel_id=1, source_target_pairs={{0,1},{1,0},{2,3},{3,2},{4,5},{5,4},{6,7},{7,6},{8,9},{9,8},{10,11... | collective-permute-start | bytes 786440 | tf_op jit(solution)/shard_map/ppermute | solution.py:35
  76.8 3.1 %collective-permute-start.23 = (bf16[32,4096]{1,0:T(8,128)(2,1)S(1)}, bf16[32,4096]{1,0:T(8,128)(2,1)S(1)}, u32[]{:S(2)}, u32[]{:S(2)}) collective-permute-start(bf16[32,4096]{1,0:T(8,128)(2,1)S(1)} %collective-permute-done.19.refs_8_), channel_id=1, source_target_pairs={{0,1},{1,0},{2,3},{3,2},{4,5},{5,4},{6,7},{7,6},{8,9},{9,8},{10,11... | collective-permute-start | bytes 786440 | tf_op jit(solution)/shard_map/ppermute | solution.py:35
  78.7 1.5 %collective-permute-start.22 = (bf16[32,4096]{1,0:T(8,128)(2,1)S(1)}, bf16[32,4096]{1,0:T(8,128)(2,1)S(1)}, u32[]{:S(2)}, u32[]{:S(2)}) collective-permute-start(bf16[32,4096]{1,0:T(8,128)(2,1)S(1)} %collective-permute-done.18.refs_7_), channel_id=1, source_target_pairs={{0,1},{1,0},{2,3},{3,2},{4,5},{5,4},{6,7},{7,6},{8,9},{9,8},{10,11... | collective-permute-start | bytes 786440 | tf_op jit(solution)/shard_map/ppermute | solution.py:35
  78.7 1.9 %collective-permute-start.21 = (bf16[32,4096]{1,0:T(8,128)(2,1)S(1)}, bf16[32,4096]{1,0:T(8,128)(2,1)S(1)}, u32[]{:S(2)}, u32[]{:S(2)}) collective-permute-start(bf16[32,4096]{1,0:T(8,128)(2,1)S(1)} %collective-permute-done.17.refs_6_), channel_id=1, source_target_pairs={{0,1},{1,0},{2,3},{3,2},{4,5},{5,4},{6,7},{7,6},{8,9},{9,8},{10,11... | collective-permute-start | bytes 786440 | tf_op jit(solution)/shard_map/ppermute | solution.py:35
  79.2 1.8 %collective-permute-start.20 = (bf16[32,4096]{1,0:T(8,128)(2,1)S(1)}, bf16[32,4096]{1,0:T(8,128)(2,1)S(1)}, u32[]{:S(2)}, u32[]{:S(2)}) collective-permute-start(bf16[32,4096]{1,0:T(8,128)(2,1)S(1)} %collective-permute-done.16.refs_5_), channel_id=1, source_target_pairs={{0,1},{1,0},{2,3},{3,2},{4,5},{5,4},{6,7},{7,6},{8,9},{9,8},{10,11... | collective-permute-start | bytes 786440 | tf_op jit(solution)/shard_map/ppermute | solution.py:35
